TPU v7x, 512 devices: a whole 4x4x16 slice. The times are simulated.
512 devices in a mesh: lat: 64 (over z_lo, x, core), wid: 8 (over z_hi, y).
Axes of the slice: x: 4, y: 4, z: 16 (z_hi: 2, z_lo: 8; z = z_hi * 8 + z_lo), core: 2. Of those that a mesh axis runs over, the one named last changes fastest.
Arguments:
- activations: bfloat16 [8192, 4096], P('lat', 'wid'), may hold values from -1.1953125 to 1.1953125
- block_ids: int32 [8192, 4], P('lat'), may hold values from 0 to 511, all different within a row; in each aligned block of 128 rows (0 to 127, 128 to 255, ...) at most 2 rows name the same one
- alive_tallies: int32 [8192], P('lat'), may hold values from 2 to 4
- encoder: bfloat16 [4096, 65536], P('wid', 'lat'), may hold values from -0.5 to 0.5
- encoder_bias: float32 [65536], P('lat'), may hold values from -3 to 3
- decoder: bfloat16 [65536, 4096], P('lat', 'wid'), may hold values from -3.2 to 3.2
Outputs:
- encoder_grad: bfloat16 [4096, 65536], P('wid', 'lat')
- decoder_grad: bfloat16 [65536, 4096], P('lat', 'wid')
- bias_grad: float32 [65536], P('lat')
Inputs may be any that keep to these rules, and one draw needn't show every extreme that they name: `block_ids`: the 4 ids of a row are distinct. Among the 128 rows of one index of lat no id stands more than 2 times, and some id stands exactly 2 times.
All inputs are finite; a program needn't handle non-finite values.
Results may differ from a plain program's by a relative error of at most 0.009.
Values may be sent and summed in bfloat16 or wider, within the bound.
A program may use at most 64 MiB of HBM per device.

v0:
```python
import jax
import jax.numpy as jnp
from jax import lax
from jax.sharding import PartitionSpec as P

BS = 128


epsilon = 1e-06


def activate(values):
    return jax.nn.gelu(values, approximate=True)


def body(activations, block_ids, alive_tallies, encoder, encoder_bias, decoder):
    rows_dev, features = activations.shape
    blocks_per_row = block_ids.shape[1]
    lat_size = lax.axis_size("lat")
    local_blocks = encoder.shape[1] // BS
    all_blocks = local_blocks * lat_size
    slot_capacity = max(2, 2 * rows_dev * blocks_per_row // all_blocks)
    layer_height = lat_size * slot_capacity
    grand_total = local_blocks * layer_height
    place_number = rows_dev * blocks_per_row
    flat_blocks = block_ids.reshape(place_number)
    slot_order = jnp.arange(place_number, dtype=jnp.int32)
    sorted_order = jnp.argsort(flat_blocks, stable=True)
    sorted_blocks = flat_blocks[sorted_order]
    run_starts = jnp.searchsorted(sorted_blocks, sorted_blocks, side="left")
    slot_ordering = (
        jnp.zeros((place_number,), jnp.int32).at[sorted_order].set(slot_order - run_starts)
    )
    group_alive_flags = (
        jnp.arange(blocks_per_row, dtype=jnp.int32)[None, :] < alive_tallies[:, None]
    ).reshape(place_number)
    owner_device = flat_blocks // local_blocks
    offset_within_block = flat_blocks % local_blocks
    slot_location = jnp.where(
        group_alive_flags,
        offset_within_block * layer_height + owner_device * slot_capacity + slot_ordering,
        grand_total,
    )
    source_row = (
        jnp.full((grand_total + 1,), rows_dev, jnp.int32)
        .at[slot_location]
        .set(slot_order // blocks_per_row)[:grand_total]
    )
    outgoing = jnp.take(activations, source_row, axis=0, mode="fill", fill_value=0).reshape(
        local_blocks, layer_height, features
    )
    live_flags = (
        jnp.zeros((grand_total + 1,), jnp.bfloat16)
        .at[slot_location]
        .set(1.0)[:grand_total]
        .reshape(local_blocks, layer_height)
    )
    decoder_wide = decoder.astype(jnp.float32)
    local_sq = jnp.sum(jnp.square(decoder_wide), axis=1)
    encoder_blocks = encoder.reshape(features, local_blocks, BS)
    row_sq = lax.psum(local_sq, "wid")
    incoming_rows, live_in = (
        lax.all_to_all(outgoing, "lat", split_axis=1, concat_axis=1, tiled=True),
        lax.all_to_all(live_flags, "lat", split_axis=1, concat_axis=1, tiled=True),
    )
    partial_pre = jnp.einsum(
        "aec,caw->aew", incoming_rows, encoder_blocks, preferred_element_type=jnp.float32
    )
    summed_pre = lax.psum(partial_pre, "wid")
    preact = summed_pre + encoder_bias.reshape(local_blocks, 1, BS)
    live_mask = live_in.astype(jnp.float32)[:, :, None]
    gated, pullback = jax.vjp(activate, preact)
    latent_codes = (gated * live_mask).astype(jnp.bfloat16)
    row_norm = jnp.sqrt(row_sq + epsilon)
    unit_rows = (decoder_wide / row_norm[:, None]).astype(jnp.bfloat16)
    normalized_blocks = unit_rows.reshape(local_blocks, BS, features)
    partial_terms = jnp.einsum(
        "jkr,jrs->jks", latent_codes, normalized_blocks, preferred_element_type=jnp.float32
    ).astype(jnp.bfloat16)
    returned = lax.all_to_all(partial_terms, "lat", split_axis=1, concat_axis=1, tiled=True)
    slot_terms = jnp.take(
        returned.reshape(grand_total, features), slot_location, axis=0, mode="fill", fill_value=0
    )
    recon = jnp.sum(
        slot_terms.astype(jnp.float32).reshape(rows_dev, blocks_per_row, features), axis=1
    )
    residual = (recon - activations.astype(jnp.float32)).astype(jnp.bfloat16)
    resid_send = jnp.take(residual, source_row, axis=0, mode="fill", fill_value=0).reshape(
        local_blocks, layer_height, features
    )
    residual_input = lax.all_to_all(resid_send, "lat", split_axis=1, concat_axis=1, tiled=True)
    partial_dcode = jnp.einsum(
        "zea,zxa->zex", residual_input, normalized_blocks, preferred_element_type=jnp.float32
    )
    unprojected_gradient = jnp.einsum(
        "ekc,ekv->ecv", latent_codes, residual_input, preferred_element_type=jnp.float32
    )
    unit_wide = normalized_blocks.astype(jnp.float32)
    partial_along = jnp.sum(unprojected_gradient * unit_wide, axis=2)
    dcode, along = lax.psum((partial_dcode, partial_along), "wid")
    dpre = pullback(dcode)[0] * live_mask
    bias_grad = jnp.sum(dpre, axis=1).reshape(local_blocks * BS)
    half_preact_gradient = dpre.astype(jnp.bfloat16)
    encoder_grad = (
        jnp.einsum(
            "kiy,kif->ykf", incoming_rows, half_preact_gradient, preferred_element_type=jnp.float32
        )
        .reshape(features, local_blocks * BS)
        .astype(jnp.bfloat16)
    )
    decoder_grad = (
        (
            (unprojected_gradient - along[:, :, None] * unit_wide)
            / row_norm.reshape(local_blocks, BS, 1)
        )
        .astype(jnp.bfloat16)
        .reshape(local_blocks * BS, features)
    )
    return (encoder_grad, decoder_grad, bias_grad)


def solution(mesh):
    return jax.shard_map(
        body,
        mesh=mesh,
        in_specs=(
            P("lat", "wid"),
            P("lat", None),
            P("lat"),
            P("wid", "lat"),
            P("lat"),
            P("lat", "wid"),
        ),
        out_specs=(P("wid", "lat"), P("lat", "wid"), P("lat")),
        check_vma=False,
    )
```

profile of v0, /device:TPU:1, one launch (start us, length us, event | category | flops | bytes accessed | tf_op | source)
XLA Modules:
  0.0 612.2 jit_solution(6032776288087941501)
XLA Ops:
  9.1 3.8 sort.17
  16.3 35.9 %while.25 = (s32[]{:T(128)}, u32[512]{0:T(512)S(1)}, u32[512]{0:T(512)S(1)}, s32[512]{0:T(512)S(1)}, s32[]{:T(128)}, /*index=5*/s32[]{:T(128)}, s32[]{}) while((s32[]{:T(128)}, u32[512]{0:T(512)S(1)}, u32[512]{0:T(512)S(1)}, s32[512]{0:T(512)S(1)}, s32[]{:T(128)}, /*index=5*/s32[]{:T(128)}, s32[]{}) %tuple.51), condition=%wide.region_2.3_spmd.clone, body=%wide.region_1.2_spmd.clone.sunk | while | flops 10244 | bytes 40045 | solution.py:30
  16.4 3.5 gather_fusion
  23.6 3.5 gather_fusion
  27.1 3.5 gather_fusion
  30.7 3.5 gather_fusion
  34.3 3.5 gather_fusion
  37.9 3.5 gather_fusion
  41.5 3.5 gather_fusion
  57.2 4.0 gather_fusion.3
  63.0 17.0 %all-to-all-start = ((bf16[8,128,512]{2,0,1:T(8,128)(2,1)}), bf16[8,128,512]{2,0,1:T(8,128)(2,1)S(1)}, u32[]{:S(2)}, u32[]{:S(2)}) async-start(bf16[8,128,512]{2,0,1:T(8,128)(2,1)} %copy.21), calls=%async_computation | async-start | bytes 2097152 | tf_op jit(solution)/shard_map/all_to_all | solution.py:63
  80.0 3.8 scatter_custom_fusion.2
  85.4 42.6 %psum.29 = f32[1024]{0:T(1024)S(1)} all-reduce(f32[1024]{0:T(1024)S(1)} %fusion), channel_id=1, replica_groups=mesh['lat'=64,'wid'=8] {'wid'}, use_global_device_ids=true, to_apply=%region_8.10 | all-reduce | flops 1024 | bytes 8192 | tf_op jit(solution)/shard_map/psum | solution.py:61
  128.1 4.3 all-to-all-done
  132.3 33.2 %all-to-all-start.1 = ((bf16[8,64,2]{0,2,1:T(2,128)(2,1)}), bf16[8,64,2]{0,2,1:T(2,128)(2,1)S(1)}, u32[]{:S(2)}, u32[]{:S(2)}) async-start(bf16[8,64,2]{0,2,1:T(2,128)(2,1)} %copy.24), calls=%async_computation.1 | async-start | bytes 65536 | tf_op jit(solution)/shard_map/all_to_all | solution.py:64
  167.7 10.1 %all-to-all-done.1 = bf16[8,64,2]{0,2,1:T(2,128)(2,1)S(1)} async-done(((bf16[8,64,2]{0,2,1:T(2,128)(2,1)}), bf16[8,64,2]{0,2,1:T(2,128)(2,1)S(1)}, u32[]{:S(2)}, u32[]{:S(2)}) %all-to-all-start.1) | async-done | bytes 2080 | tf_op jit(solution)/shard_map/all_to_all | solution.py:64
  177.9 137.6 %all-reduce.3.cloned.1.call-done = f32[8,128,128]{2,1,0:T(8,128)} async-done(((f32[8,128,128]{2,1,0:T(8,128)}), f32[8,128,128]{2,1,0:T(8,128)}) %all-reduce.3.cloned.1.call-update) | async-done | bytes 524304 | tf_op jit(solution)/shard_map/psum | solution.py:69
  318.6 12.6 %all-to-all-start.2 = ((bf16[8,128,512]{2,0,1:T(8,128)(2,1)}), bf16[8,128,512]{2,0,1:T(8,128)(2,1)}, u32[]{:S(2)}, u32[]{:S(2)}) async-start(bf16[8,128,512]{2,0,1:T(8,128)(2,1)} %copy.26), calls=%async_computation.2 | async-start | bytes 2097152 | tf_op jit(solution)/shard_map/all_to_all | solution.py:80
  331.4 51.2 %all-to-all-done.2 = bf16[8,128,512]{2,0,1:T(8,128)(2,1)} async-done(((bf16[8,128,512]{2,0,1:T(8,128)(2,1)}), bf16[8,128,512]{2,0,1:T(8,128)(2,1)}, u32[]{:S(2)}, u32[]{:S(2)}) %all-to-all-start.2) | async-done | bytes 1048608 | tf_op jit(solution)/shard_map/all_to_all | solution.py:80
  388.8 4.0 gather_fusion.4
  393.6 59.1 %all_to_all.24 = bf16[8,128,512]{2,0,1:T(8,128)(2,1)S(1)} all-to-all(bf16[8,128,512]{2,0,1:T(8,128)(2,1)S(1)} %copy.28), channel_id=1, replica_groups=mesh['lat'=64,'wid'=8] {'lat'}, dimensions={1} | all-to-all | bytes 2097152 | tf_op jit(solution)/shard_map/all_to_all | solution.py:91
  454.9 3.9 fusion.2
  458.8 39.0 %psum.31 = f32[8,128]{1,0:T(8,128)S(1)} all-reduce(f32[8,128]{1,0:T(8,128)S(1)} %get-tuple-element.116), channel_id=1, replica_groups=mesh['lat'=64,'wid'=8] {'wid'}, use_global_device_ids=true, to_apply=%region_12.14 | all-reduce | flops 1024 | bytes 8192 | tf_op jit(solution)/shard_map/psum | solution.py:100
  500.7 99.2 %all-reduce.5.cloned.1.call-done = f32[8,128,128]{2,1,0:T(8,128)} async-done(((f32[8,128,128]{2,1,0:T(8,128)}), f32[8,128,128]{2,1,0:T(8,128)}) %all-reduce.5.cloned.1.call-update) | async-done | bytes 524304 | tf_op jit(solution)/shard_map/psum | solution.py:100
  (117 shorter events, 47.6 us)
Async XLA Ops:
  7.2 158.6 %copy-start = (bf16[512,1024]{1,0:T(8,128)(2,1)S(1)}, bf16[512,1024]{1,0:T(8,128)(2,1)}, u32[]{:S(2)}) copy-start(bf16[512,1024]{1,0:T(8,128)(2,1)} %param.13) | copy-start | bytes 3145732
  16.3 40.9 %copy-start.1 = (bf16[128,512]{1,0:T(8,128)(2,1)S(1)}, bf16[128,512]{1,0:T(8,128)(2,1)}, u32[]{:S(2)}) copy-start(bf16[128,512]{1,0:T(8,128)(2,1)} %param.10) | copy-start | bytes 393220
  61.4 23.8 %copy-start.2 = (bf16[1024,512]{1,0:T(8,128)(2,1)S(1)}, bf16[1024,512]{1,0:T(8,128)(2,1)}, u32[]{:S(2)}) copy-start(bf16[1024,512]{1,0:T(8,128)(2,1)} %param.15) | copy-start | bytes 3145732
  63.0 69.3 %all-to-all-start = ((bf16[8,128,512]{2,0,1:T(8,128)(2,1)}), bf16[8,128,512]{2,0,1:T(8,128)(2,1)S(1)}, u32[]{:S(2)}, u32[]{:S(2)}) async-start(bf16[8,128,512]{2,0,1:T(8,128)(2,1)} %copy.21), calls=%async_computation | async-start | bytes 2097152 | tf_op jit(solution)/shard_map/all_to_all | solution.py:63
  132.3 35.1 %copy-start.6 = (bf16[8,128,512]{2,0,1:T(8,128)(2,1)}, bf16[8,128,512]{2,0,1:T(8,128)(2,1)S(1)}, u32[]{:S(2)}) copy-start(bf16[8,128,512]{2,0,1:T(8,128)(2,1)S(1)} %all-to-all-done) | copy-start | bytes 3145732
  132.3 45.5 %all-to-all-start.1 = ((bf16[8,64,2]{0,2,1:T(2,128)(2,1)}), bf16[8,64,2]{0,2,1:T(2,128)(2,1)S(1)}, u32[]{:S(2)}, u32[]{:S(2)}) async-start(bf16[8,64,2]{0,2,1:T(2,128)(2,1)} %copy.24), calls=%async_computation.1 | async-start | bytes 65536 | tf_op jit(solution)/shard_map/all_to_all | solution.py:64
  165.5 150.0 %all-reduce.3.cloned.1.call-start = ((), (), s32[]{:S(2)}) async-start(), calls=%async_computation.4 | async-start | bytes 1048576 | tf_op jit(solution)/shard_map/psum | solution.py:69
  167.4 148.1 %copy-start.7 = (f32[1024]{0:T(1024)S(1)}, f32[1024]{0:T(1024)}, u32[]{:S(2)}) copy-start(f32[1024]{0:T(1024)} %param.14) | copy-start | bytes 12292
  318.6 64.1 %all-to-all-start.2 = ((bf16[8,128,512]{2,0,1:T(8,128)(2,1)}), bf16[8,128,512]{2,0,1:T(8,128)(2,1)}, u32[]{:S(2)}, u32[]{:S(2)}) async-start(bf16[8,128,512]{2,0,1:T(8,128)(2,1)} %copy.26), calls=%async_computation.2 | async-start | bytes 2097152 | tf_op jit(solution)/shard_map/all_to_all | solution.py:80
  331.2 268.7 %all-reduce.5.cloned.1.call-start = ((), (), s32[]{:S(2)}) async-start(), calls=%async_computation.5 | async-start | bytes 1048576 | tf_op jit(solution)/shard_map/psum | solution.py:100
  452.6 1.0 copy-start.4
  454.9 42.9 %copy-start.3 = (bf16[1024,512]{1,0:T(8,128)(2,1)S(1)}, bf16[1024,512]{1,0:T(8,128)(2,1)}, u32[]{:S(2)}) copy-start(bf16[1024,512]{1,0:T(8,128)(2,1)} %param.15) | copy-start | bytes 3145732
  497.8 102.1 %copy-start.5 = (f32[8,128,128]{2,1,0:T(8,128)S(1)}, f32[8,128,128]{2,1,0:T(8,128)}, u32[]{:S(2)}) copy-start(f32[8,128,128]{2,1,0:T(8,128)} %all-reduce.3.cloned.1.call-done) | copy-start | bytes 1572868
Sparse Core Ops, SparseCore 0:
  169.8 145.6 all-reduce.2
  455.0 144.8 all-reduce.4
where the time goes:
time: 618 us; the launch traced here: 612 us
  waiting for transfers between devices  302 us (49%)
  blocking collectives  141 us (23%)
  local copies, waits for them, and re-layouts  68.9 us (11%)
  starting transfers between devices  63.1 us (10%)
  between operations  14.4 us (2%)
  other arithmetic  11.8 us (2%)
  matrix products  10.4 us (2%)
    psum x1, waiting for transfers between devices, body(): summed_pre = lax.psum(partial_pre, 'wid')  138 us
    psum x1, waiting for transfers between devices, body(): dcode, along = lax.psum((partial_dcode, partial_along), 'wid')  99.2 us
    all_to_all x1, blocking collectives, body(): lax.all_to_all(resid_send, 'lat', split_axis=1, concat_axis=1, tiled=True)  59.1 us
    all_to_all x1, waiting for transfers between devices, body(): lax.all_to_all(partial_terms, 'lat', split_axis=1, concat_axis=1, tiled=T...  51.2 us
    psum x1, blocking collectives, body(): row_sq = lax.psum(local_sq, 'wid')  42.6 us
    psum x1, blocking collectives, body(): dcode, along = lax.psum((partial_dcode, partial_along), 'wid')  39 us
    gather x10, local copies, waits for them, and re-layouts, body(): run_starts = jnp.searchsorted(sorted_blocks, sorted_blocks, side='left')  34.9 us
    all_to_all x1, starting transfers between devices, body(): lax.all_to_all(live_flags, 'lat', split_axis=1, concat_axis=1, tiled=True)  33.2 us
  transfers between devices with their start and end apart: 5, of which 5 were waited for; matrix products, arithmetic and copies ran while one was open for 2% of the time, Pallas kernels for 0%

commit v1 on v0

v1 whole, which is shorter than its diff:
```python
import functools

import jax
import jax.numpy as jnp
from jax import lax
from jax.experimental import pallas as pl
from jax.experimental.pallas import tpu as pltpu
from jax.sharding import PartitionSpec as P

BS = 128
EPS = 1e-06
C0 = 0.7978845608
C1 = 0.044715
FILLER = 2.0
MESH = pl.DeviceIdType.MESH


def gelu(v):
    return 0.5 * v * (1.0 + jnp.tanh(C0 * (v + C1 * v * v * v)))


def gelu_slope(v):
    t = jnp.tanh(C0 * (v + C1 * v * v * v))
    return 0.5 * (1.0 + t) + 0.5 * v * (1.0 - t * t) * C0 * (1.0 + 3.0 * C1 * v * v)


def wid_place():
    me = lax.axis_index("wid")
    hi, y = me // 4, me % 4
    partner = (1 - hi) * 4 + y
    peers = [hi * 4 + (y + d) % 4 for d in (1, 2, 3)]
    return hi, y, partner, peers


def greet(others):
    barrier = pltpu.get_barrier_semaphore()
    for other in others:
        pl.semaphore_signal(barrier, inc=1, device_id={"wid": other}, device_id_type=MESH)
    pl.semaphore_wait(barrier, len(others))


def send(src, dst, send_sem, recv_sem, to):
    copy = pltpu.make_async_remote_copy(
        src_ref=src,
        dst_ref=dst,
        send_sem=send_sem,
        recv_sem=recv_sem,
        device_id={"wid": to},
        device_id_type=MESH,
    )
    copy.start()
    return copy


def scatter_sums(part_ref, got_y, mine, got_z, sems, place):
    hi, y, partner, peers = place
    copies = [
        send(part_ref.at[:, (y + d) % 4], got_y.at[d - 1], sems.at[0, d - 1], sems.at[1, d - 1], peers[d - 1])
        for d in (1, 2, 3)
    ]
    for copy in copies:
        copy.wait()

    def total(h):
        s = part_ref[h, y].astype(jnp.float32)
        for d in range(3):
            s = s + got_y[d, h].astype(jnp.float32)
        return s

    mine[...] = total(1 - hi).astype(mine.dtype)
    copy = send(mine, got_z, sems.at[0, 3], sems.at[1, 3], partner)
    own = total(hi)
    copy.wait()
    return own + got_z[...].astype(jnp.float32)


def gather_start(out_ref, sems, base, place):
    hi, y, partner, peers = place
    block = out_ref.at[hi, y]
    far = send(block, block, sems.at[0, base], sems.at[1, base], partner)
    near = [
        send(block, block, sems.at[0, base + d], sems.at[1, base + d], peers[d - 1]) for d in (1, 2, 3)
    ]
    return far, near


def gather_pass(out_ref, sems, base, far, place):
    hi, y, partner, peers = place
    far.wait()
    block = out_ref.at[1 - hi, y]
    return [
        send(block, block, sems.at[0, base + 3 + d], sems.at[1, base + 3 + d], peers[d - 1])
        for d in (1, 2, 3)
    ]


def forward_kernel(part_ref, sq_ref, bias_ref, live_ref, codes_ref, pre_ref, own_ref, row_ref,
                   got_y, mine, got_z, sq_y, sq_mine, sq_z, sems):
    place = wid_place()
    hi, y, partner, peers = place
    greet([partner] + peers)
    sq_copies = [
        send(sq_ref, sq_y.at[d - 1], sems.at[0, 10 + d], sems.at[1, 10 + d], peers[d - 1]) for d in (1, 2, 3)
    ]
    for copy in sq_copies:
        copy.wait()
    sq_mine[...] = sq_ref[...] + sq_y[0] + sq_y[1] + sq_y[2]
    sq_far = send(sq_mine, sq_z, sems.at[0, 14], sems.at[1, 14], partner)
    preact = scatter_sums(part_ref, got_y, mine, got_z, sems, place) + bias_ref[...]
    pre_ref[...] = preact
    codes = (gelu(preact) * live_ref[...]).astype(jnp.bfloat16)
    own_ref[...] = codes
    codes_ref[hi, y] = codes
    far, near = gather_start(codes_ref, sems, 4, place)
    sq_far.wait()
    row_ref[...] = sq_mine[...] + sq_z[...]
    late = gather_pass(codes_ref, sems, 4, far, place)
    for copy in near + late:
        copy.wait()


def backward_kernel(part_ref, pre_ref, own_ref, live_ref, dpre_ref, small_ref, got_y, mine, got_z, sems):
    place = wid_place()
    hi, y, partner, peers = place
    greet([partner] + peers)
    dcode = scatter_sums(part_ref, got_y, mine, got_z, sems, place)
    dpre = dcode * gelu_slope(pre_ref[...]) * live_ref[...]
    dpre_ref[hi, y] = dpre.astype(jnp.bfloat16)
    far, near = gather_start(dpre_ref, sems, 4, place)
    along = jnp.sum(own_ref[...].astype(jnp.float32) * dcode, axis=0, keepdims=True)
    bias_grad = jnp.sum(dpre, axis=0, keepdims=True)
    row = lax.broadcasted_iota(jnp.int32, (8, BS), 0)
    small_ref[hi, y] = jnp.where(row == 0, along, bias_grad)
    small_far, small_near = gather_start(small_ref, sems, 11, place)
    late = gather_pass(dpre_ref, sems, 4, far, place)
    small_late = gather_pass(small_ref, sems, 11, small_far, place)
    for copy in near + late + small_near + small_late:
        copy.wait()


def vmem(n):
    return [pl.BlockSpec(memory_space=pltpu.VMEM)] * n


def sum_scratch(slots):
    return [
        pltpu.VMEM((3, 2, slots, BS), jnp.bfloat16),
        pltpu.VMEM((slots, BS), jnp.bfloat16),
        pltpu.VMEM((slots, BS), jnp.bfloat16),
    ]


def forward_sums(part, sq, bias, live):
    slots = part.shape[2]
    return pl.pallas_call(
        forward_kernel,
        out_shape=(
            jax.ShapeDtypeStruct((2, 4, slots, BS), jnp.bfloat16),
            jax.ShapeDtypeStruct((slots, BS), jnp.float32),
            jax.ShapeDtypeStruct((slots, BS), jnp.bfloat16),
            jax.ShapeDtypeStruct((8, BS), jnp.float32),
        ),
        in_specs=vmem(4),
        out_specs=tuple(vmem(4)),
        scratch_shapes=sum_scratch(slots)
        + [
            pltpu.VMEM((3, 8, BS), jnp.float32),
            pltpu.VMEM((8, BS), jnp.float32),
            pltpu.VMEM((8, BS), jnp.float32),
            pltpu.SemaphoreType.DMA((2, 15)),
        ],
        compiler_params=pltpu.CompilerParams(collective_id=0, has_side_effects=True),
        name="forward_sums",
    )(part, sq, bias, live)


def backward_sums(part, pre, own, live):
    slots = part.shape[2]
    return pl.pallas_call(
        backward_kernel,
        out_shape=(
            jax.ShapeDtypeStruct((2, 4, slots, BS), jnp.bfloat16),
            jax.ShapeDtypeStruct((2, 4, 8, BS), jnp.float32),
        ),
        in_specs=vmem(4),
        out_specs=tuple(vmem(2)),
        scratch_shapes=sum_scratch(slots) + [pltpu.SemaphoreType.DMA((2, 18))],
        compiler_params=pltpu.CompilerParams(collective_id=1, has_side_effects=True),
        name="backward_sums",
    )(part, pre, own, live)


def to_owner(x, lat):
    features = x.shape[-1]
    x = lax.all_to_all(x.reshape(lat, 16, features), "lat", split_axis=0, concat_axis=0, tiled=True)
    return x.reshape(lat, 8, 2, features).transpose(1, 0, 2, 3).reshape(8, lat * 2, features)


def to_row(x, lat):
    features = x.shape[-1]
    x = x.reshape(8, lat, 2, features).transpose(1, 0, 2, 3).reshape(lat, 16, features)
    x = lax.all_to_all(x, "lat", split_axis=0, concat_axis=0, tiled=True)
    return x.reshape(lat * 16, features)


def body(activations, block_ids, alive_tallies, encoder, encoder_bias, decoder):
    rows, features = activations.shape
    slots = block_ids.shape[1]
    lat = lax.axis_size("lat")
    wid = lax.axis_index("wid")
    positions = lat * 16
    f32 = jnp.float32

    flat = block_ids.reshape(rows * slots)
    order = jnp.arange(rows * slots, dtype=jnp.int32)
    earlier = (flat[:, None] == flat[None, :]) & (order[None, :] < order[:, None])
    rank = jnp.sum(earlier.astype(jnp.int32), axis=1).reshape(rows, slots)
    alive = jnp.arange(slots, dtype=jnp.int32)[None, :] < alive_tallies[:, None]
    position = jnp.where(alive, block_ids * 2 + rank, -1)
    spots = jnp.arange(positions, dtype=jnp.int32)[:, None]
    place = spots == position[:, 0][None, :]
    for j in range(1, slots):
        place = place | (spots == position[:, j][None, :])
    filled = jnp.any(place, axis=1, keepdims=True)
    place = place.astype(jnp.bfloat16)

    outgoing = jnp.dot(place, activations, preferred_element_type=f32)
    outgoing = jnp.where(filled, outgoing, FILLER).astype(jnp.bfloat16)
    incoming = to_owner(outgoing, lat)
    live = (incoming[:, :, 0] < 1.5).astype(f32)
    own_live = jnp.broadcast_to(
        lax.dynamic_index_in_dim(live, wid, 0, keepdims=False)[:, None], (lat * 2, BS)
    )

    decoder_wide = decoder.astype(f32)
    local_sq = jnp.sum(jnp.square(decoder_wide), axis=1).reshape(8, BS)
    encoder_blocks = encoder.reshape(features, 8, BS)
    partial_pre = jnp.einsum(
        "aec,caw->aew", incoming, encoder_blocks, preferred_element_type=f32
    ).astype(jnp.bfloat16)
    own_bias = lax.dynamic_index_in_dim(encoder_bias.reshape(8, BS), wid, 0, keepdims=True)
    codes, own_pre, own_codes, row_sq = forward_sums(
        partial_pre.reshape(2, 4, lat * 2, BS), local_sq, own_bias, own_live
    )
    codes = codes.reshape(8, lat * 2, BS)
    row_norm = jnp.sqrt(row_sq + EPS)[:, :, None]
    unit = (decoder_wide.reshape(8, BS, features) / row_norm).astype(jnp.bfloat16)

    terms = jnp.einsum("jkr,jrs->jks", codes, unit, preferred_element_type=f32).astype(jnp.bfloat16)
    returned = to_row(terms, lat)
    recon = lax.dot_general(place, returned, (((0,), (0,)), ((), ())), preferred_element_type=f32)
    residual = (recon - activations.astype(f32)).astype(jnp.bfloat16)
    resid_send = jnp.dot(place, residual, preferred_element_type=f32).astype(jnp.bfloat16)
    resid_in = to_owner(resid_send, lat)

    partial_dcode = jnp.einsum(
        "zea,zxa->zex", resid_in, unit, preferred_element_type=f32
    ).astype(jnp.bfloat16)
    dpre, small = backward_sums(
        partial_dcode.reshape(2, 4, lat * 2, BS), own_pre, own_codes, own_live
    )
    dpre = dpre.reshape(8, lat * 2, BS)
    small = small.reshape(8, 8, BS)
    raw = jnp.einsum("ekc,ekv->ecv", codes, resid_in, preferred_element_type=f32)
    along = small[:, 0, :, None]
    bias_grad = small[:, 1].reshape(8 * BS)
    encoder_grad = (
        jnp.einsum("kiy,kif->ykf", incoming, dpre, preferred_element_type=f32)
        .reshape(features, 8 * BS)
        .astype(jnp.bfloat16)
    )
    decoder_grad = (
        ((raw - along * unit.astype(f32)) / row_norm).astype(jnp.bfloat16).reshape(8 * BS, features)
    )
    return encoder_grad, decoder_grad, bias_grad


def solution(mesh):
    return jax.shard_map(
        body,
        mesh=mesh,
        in_specs=(
            P("lat", "wid"),
            P("lat", None),
            P("lat"),
            P("wid", "lat"),
            P("lat"),
            P("lat", "wid"),
        ),
        out_specs=(P("wid", "lat"), P("lat", "wid"), P("lat")),
        check_vma=False,
    )
```

time: 618 us -> 293 us (0.47)
  waiting for transfers between devices: 302 us -> 49.4 us
  Pallas kernels: 0 us -> 61 us
  local copies, waits for them, and re-layouts: 68.9 us -> 19.1 us
  starting transfers between devices: 63.1 us -> 17.2 us
  blocking collectives: 141 us -> 123 us
  between operations: 14.4 us -> 0.77 us
  other arithmetic: 11.8 us -> 4.48 us
    psum x2 -> x0, waiting for transfers between devices: 237 us -> none  [the longest x1 138 us: body(): summed_pre = lax.psum(partial_pre, 'wid')]
    psum x2 -> x0, blocking collectives: 81.6 us -> none  [the longest x1 42.6 us: body(): row_sq = lax.psum(local_sq, 'wid')]
    all_to_all x1 -> x2, blocking collectives: 59.1 us -> 123 us  [the longest x1 63.6 us: to_row(): x = lax.all_to_all(x, 'lat', split_axis=0, concat_axis=0, tiled=True)]
    pallas_call x0 -> x2, Pallas kernels: none -> 60.9 us  [the longest x1 32.8 us: forward_sums(): pl.pallas_call(forward_kernel, out_shape=(jax.ShapeDtypeStruct((2, 4, slo...]
    gather x15 -> x0, local copies, waits for them, and re-layouts: 50.1 us -> none  [the longest x10 34.9 us: body(): run_starts = jnp.searchsorted(sorted_blocks, sorted_blocks, side='left')]
    all_to_all x3 -> x1, starting transfers between devices: 62.9 us -> 17.2 us  [to_owner(): lax.all_to_all(x.reshape(lat, 16, features), 'lat', split_axis=0, concat_...]
    all_to_all x3 -> x1, waiting for transfers between devices: 65.6 us -> 49.4 us  [to_owner(): lax.all_to_all(x.reshape(lat, 16, features), 'lat', split_axis=0, concat_...]
    reshape x3 -> x11, local copies, waits for them, and re-layouts: 2.23 us -> 13.4 us  [the longest x6 9 us: to_owner(): x.reshape(lat, 8, 2, features).transpose(1, 0, 2, 3)]
  transfers between devices with their start and end apart: 5 -> 1, of which waited for: 5 -> 1; matrix products, arithmetic and copies ran while one was open for 2% -> 1% of each run, Pallas kernels for 0% -> 0%
where the time goes in v1:
time: 293 us; the launch traced here: 288 us
  blocking collectives  123 us (42%)
  Pallas kernels  61 us (21%)
  waiting for transfers between devices  49.4 us (17%)
  local copies, waits for them, and re-layouts  19.1 us (7%)
  starting transfers between devices  17.2 us (6%)
  matrix products  13.6 us (5%)
  other arithmetic  4.48 us (2%)
    all_to_all x1, blocking collectives, to_row(): x = lax.all_to_all(x, 'lat', split_axis=0, concat_axis=0, tiled=True)  63.6 us
    all_to_all x1, blocking collectives, to_owner(): lax.all_to_all(x.reshape(lat, 16, features), 'lat', split_axis=0, concat_...  59.4 us
    all_to_all x1, waiting for transfers between devices, to_owner(): lax.all_to_all(x.reshape(lat, 16, features), 'lat', split_axis=0, concat_...  49.4 us
    pallas_call x1, Pallas kernels, forward_sums(): pl.pallas_call(forward_kernel, out_shape=(jax.ShapeDtypeStruct((2, 4, slo...  32.8 us
    pallas_call x1, Pallas kernels, backward_sums(): pl.pallas_call(backward_kernel, out_shape=(jax.ShapeDtypeStruct((2, 4, sl...  28.2 us
    all_to_all x1, starting transfers between devices, to_owner(): lax.all_to_all(x.reshape(lat, 16, features), 'lat', split_axis=0, concat_...  17.2 us
    reshape x6, local copies, waits for them, and re-layouts, to_owner(): x.reshape(lat, 8, 2, features).transpose(1, 0, 2, 3)  9 us
  transfers between devices with their start and end apart: 1, of which 1 were waited for; matrix products, arithmetic and copies ran while one was open for 1% of the time, Pallas kernels for 0%

profile of v1, /device:TPU:1, one launch (start us, length us, event | category | flops | bytes accessed | tf_op | source)
XLA Modules:
  0.0 288.4 jit_solution(12893836691099097226)
XLA Ops:
  0.6 0.9 copy.58
  3.1 2.3 select_convert_fusion
  5.4 17.2 %all-to-all-start = ((bf16[64,16,512]{2,1,0:T(8,128)(2,1)}), bf16[64,16,512]{2,1,0:T(8,128)(2,1)S(1)}, u32[]{:S(2)}, u32[]{:S(2)}) async-start(bf16[64,16,512]{2,1,0:T(8,128)(2,1)} %bitcast.59), calls=%async_computation | async-start | bytes 2097152 | tf_op jit(solution)/shard_map/all_to_all | solution.py:195
  22.6 1.2 constant_dynamic-slice_fusion.bias_ref
  23.8 0.9 multiply_reduce_fusion
  24.6 49.4 %all-to-all-done = bf16[64,16,512]{2,1,0:T(8,128)(2,1)S(1)} async-done(((bf16[64,16,512]{2,1,0:T(8,128)(2,1)}), bf16[64,16,512]{2,1,0:T(8,128)(2,1)S(1)}, u32[]{:S(2)}, u32[]{:S(2)}) %all-to-all-start) | async-done | bytes 1048608 | tf_op jit(solution)/shard_map/all_to_all | solution.py:195
  74.5 0.7 copy.78
  75.8 1.2 convolution_convert_fusion.4
  77.7 32.8 %forward_sums.1 = (bf16[2,4,128,128]{3,2,1,0:T(8,128)(2,1)}, f32[128,128]{1,0:T(8,128)}, bf16[128,128]{1,0:T(8,128)(2,1)}, f32[8,128]{1,0:T(8,128)}) custom-call(bf16[2,4,128,128]{3,2,1,0:T(8,128)(2,1)} %bitcast.65, f32[8,128]{1,0:T(8,128)} %bitcast.66, f32[1,128]{1,0:T(1,128)} %constant_dynamic-slice_fusion.bias_ref, f32[128,128]{1,0:T(8,128)} %broadcast_in_dim.35.live_ref), custom_call_target="tpu_custom_call" | custom-call | tf_op jit(solution)/shard_map/forward_sums/pallas_call | solution.py:155
  111.1 1.6 divide_convert_fusion.1
  112.7 1.4 convolution_convert_fusion.2
  114.1 2.2 reshape.95
  116.4 1.4 copy.62
  118.4 63.6 %all_to_all.15 = bf16[64,16,512]{2,1,0:T(8,128)(2,1)} all-to-all(bf16[64,16,512]{2,1,0:T(8,128)(2,1)S(1)} %copy.63), channel_id=1, replica_groups=mesh['lat'=64,'wid'=8] {'lat'}, dimensions={0} | all-to-all | bytes 2097152 | tf_op jit(solution)/shard_map/all_to_all | solution.py:202
  182.0 3.0 %convolution_convert_fusion.1 = bf16[1024,512]{1,0:T(8,128)(2,1)} fusion(bf16[1024,512]{1,0:T(8,128)(2,1)} %bitcast.60, bf16[128,512]{1,0:T(8,128)(2,1)} %param.6, s32[128]{0:T(128)S(1)} %get-tuple-element.36, s32[128]{0:T(128)S(1)} %get-tuple-element.37, s32[128]{0:T(128)S(1)} %get-tuple-element.38, s32[128]{0:T(128)S(1)} %get-tuple-element.35), kind=kOutput, calls=%fused_computation.5 | convolution fusion | flops 270991360 | bytes 2230272 | tf_op jit(solution)/shard_map/dot_general | solution.py:253
  185.0 59.4 %all_to_all.16 = bf16[64,16,512]{2,1,0:T(8,128)(2,1)} all-to-all(bf16[64,16,512]{2,1,0:T(8,128)(2,1)} %bitcast.61), channel_id=1, replica_groups=mesh['lat'=64,'wid'=8] {'lat'}, dimensions={0} | all-to-all | bytes 2097152 | tf_op jit(solution)/shard_map/all_to_all | solution.py:195
  244.4 2.2 reshape.99
  246.6 2.9 %copy.77 = bf16[64,8,2,512]{3,2,0,1:T(2,128)(2,1)} copy(bf16[64,8,2,512]{3,2,1,0:T(2,128)(2,1)} %reshape.99) | data formatting | bytes 2097152 | tf_op jit(solution)/shard_map/reshape | solution.py:196
  249.5 2.3 reshape.100
  251.8 2.4 convolution_convert_fusion.3
  254.1 28.2 %backward_sums.1 = (bf16[2,4,128,128]{3,2,1,0:T(8,128)(2,1)}, f32[2,4,8,128]{3,2,1,0:T(8,128)}) custom-call(bf16[2,4,128,128]{3,2,1,0:T(8,128)(2,1)} %bitcast.58, f32[128,128]{1,0:T(8,128)} %get-tuple-element.11.pre_ref, bf16[128,128]{1,0:T(8,128)(2,1)} %get-tuple-element.12.own_ref, f32[128,128]{1,0:T(8,128)} %broadcast_in_dim.35.live_ref), custom_call_target="tpu_custom_call" | custom-call | tf_op jit(solution)/shard_map/backward_sums/pallas_call | solution.py:179
  282.3 1.4 fusion.12
  283.8 2.8 divide_convert_fusion
  287.1 1.3 copy.67
  (23 shorter events, 5.0 us)
Async XLA Ops:
  0.6 75.2 %copy-start = (bf16[512,1024]{1,0:T(8,128)(2,1)S(1)}, bf16[512,1024]{1,0:T(8,128)(2,1)}, u32[]{:S(2)}) copy-start(bf16[512,1024]{1,0:T(8,128)(2,1)} %param.9) | copy-start | bytes 3145732
  5.4 18.4 %copy-start.1 = (bf16[1024,512]{1,0:T(8,128)(2,1)S(1)}, bf16[1024,512]{1,0:T(8,128)(2,1)}, u32[]{:S(2)}) copy-start(bf16[1024,512]{1,0:T(8,128)(2,1)} %param.11) | copy-start | bytes 3145732
  5.4 68.7 %all-to-all-start = ((bf16[64,16,512]{2,1,0:T(8,128)(2,1)}), bf16[64,16,512]{2,1,0:T(8,128)(2,1)S(1)}, u32[]{:S(2)}, u32[]{:S(2)}) async-start(bf16[64,16,512]{2,1,0:T(8,128)(2,1)} %bitcast.59), calls=%async_computation | async-start | bytes 2097152 | tf_op jit(solution)/shard_map/all_to_all | solution.py:195
  111.1 1.6 copy-start.2
  283.8 2.8 copy-start.3

commit v2 on v1

--- a/solution.py
+++ b/solution.py
@@ -12,6 +12,8 @@
 C0 = 0.7978845608
 C1 = 0.044715
 FILLER = 2.0
+LINE = 8
+PLANE = 8
 MESH = pl.DeviceIdType.MESH
 
 
@@ -190,17 +192,378 @@
     )(part, pre, own, live)
 
 
-def to_owner(x, lat):
-    features = x.shape[-1]
-    x = lax.all_to_all(x.reshape(lat, 16, features), "lat", split_axis=0, concat_axis=0, tiled=True)
-    return x.reshape(lat, 8, 2, features).transpose(1, 0, 2, 3).reshape(8, lat * 2, features)
-
-
-def to_row(x, lat):
-    features = x.shape[-1]
-    x = x.reshape(8, lat, 2, features).transpose(1, 0, 2, 3).reshape(lat, 16, features)
-    x = lax.all_to_all(x, "lat", split_axis=0, concat_axis=0, tiled=True)
-    return x.reshape(lat * 16, features)
+def lat_place():
+    me = lax.axis_index("lat")
+    return me // PLANE, me % PLANE
+
+
+def greet_lat(place):
+    z, q = place
+    barrier = pltpu.get_barrier_semaphore()
+
+    def signal(other):
+        pl.semaphore_signal(barrier, inc=1, device_id={"lat": other}, device_id_type=MESH)
+
+    for e in range(1, PLANE):
+        signal(z * PLANE + (q + e) % PLANE)
+
+    @pl.when(z > 0)
+    def _():
+        signal((z - 1) * PLANE + q)
+
+    @pl.when(z < LINE - 1)
+    def _():
+        signal((z + 1) * PLANE + q)
+
+    inner = jnp.logical_and(z > 0, z < LINE - 1)
+
+    @pl.when(inner)
+    def _():
+        pl.semaphore_wait(barrier, PLANE + 1)
+
+    @pl.when(jnp.logical_not(inner))
+    def _():
+        pl.semaphore_wait(barrier, PLANE)
+
+
+def lat_copy(src, dst, send_sem, recv_sem, z, q):
+    return pltpu.make_async_remote_copy(
+        src_ref=src,
+        dst_ref=dst,
+        send_sem=send_sem,
+        recv_sem=recv_sem,
+        device_id={"lat": z * PLANE + q},
+        device_id_type=MESH,
+    )
+
+
+def half(c, features):
+    return pl.ds(c * (features // 2), features // 2)
+
+
+def slot_matrix(local):
+    spots = lax.broadcasted_iota(jnp.int32, (BS, BS), 0).astype(jnp.float32)
+    hit = jnp.zeros((BS, BS), jnp.float32)
+    for j in range(4):
+        hit = hit + jnp.where(spots == local[j : j + 1, :], 1.0, 0.0)
+    return hit
+
+
+def swap_matrix():
+    r = lax.broadcasted_iota(jnp.int32, (BS, BS), 0)
+    col = lax.broadcasted_iota(jnp.int32, (BS, BS), 1)
+    source = ((r >> 1) & 7) * 16 + (r >> 4) * 2 + (r & 1)
+    return jnp.where(source == col, 1.0, 0.0).astype(jnp.bfloat16)
+
+
+def spread(x_ref, all_ref, pos_ref, stage, got, out_ref, line_sems, plane_sems, place, first):
+    z, q = place
+    rows = BS
+    features = x_ref.shape[1]
+
+    def line_copy(b, step, c, way, src=None):
+        src = all_ref.at[b] if src is None else src
+        return lat_copy(
+            src.at[:, half(c, features)],
+            all_ref.at[b, :, half(c, features)],
+            line_sems.at[0, way, step, c],
+            line_sems.at[1, way, step, c],
+            z + 1 - 2 * way,
+            q,
+        )
+
+    def plane_copy(b, e):
+        to = (q + e) % PLANE
+        return lat_copy(
+            stage.at[b, to], got.at[q, b], plane_sems.at[0, b, e - 1], plane_sems.at[1, b, e - 1], z, to
+        )
+
+    def select(b, ref):
+        if first:
+            code = ref[rows : rows + 8, 0:BS].astype(jnp.float32)
+            base = (z * BS).astype(jnp.float32)
+            local = code[0:4] * 8.0 + code[4:8] - base
+            pos_ref[b] = jnp.concatenate([local, local], axis=0)
+        else:
+            local = pos_ref[b]
+        hit = slot_matrix(local)
+        picked = jnp.dot(hit.astype(jnp.bfloat16), ref[0:rows, :], preferred_element_type=jnp.float32)
+        if first:
+            filled = jnp.sum(hit, axis=1, keepdims=True)
+            picked = jnp.where(filled > 0.5, picked, FILLER)
+        stage[b] = picked.astype(jnp.bfloat16).reshape(PLANE, 16, features)
+        got[q, b] = stage[b, q]
+        for e in range(1, PLANE):
+            plane_copy(b, e).start()
+
+    can_right, can_left = z < LINE - 1, z > 0
+    for c in range(2):
+        @pl.when(can_right)
+        def _():
+            line_copy(z, 0, c, 0, x_ref).start()
+
+        @pl.when(can_left)
+        def _():
+            line_copy(z, 0, c, 1, x_ref).start()
+
+    select(z, x_ref)
+
+    def advance(step, _):
+        from_left, from_right = z - step, z + step
+        for c in range(2):
+            @pl.when(from_left >= 0)
+            def _():
+                line_copy(from_left, step - 1, c, 0).wait_recv()
+
+                @pl.when(can_right)
+                def _():
+                    line_copy(from_left, step, c, 0).start()
+
+            @pl.when(from_right < LINE)
+            def _():
+                line_copy(from_right, step - 1, c, 1).wait_recv()
+
+                @pl.when(can_left)
+                def _():
+                    line_copy(from_right, step, c, 1).start()
+
+        @pl.when(from_left >= 0)
+        def _():
+            select(from_left, all_ref.at[from_left])
+
+        @pl.when(from_right < LINE)
+        def _():
+            select(from_right, all_ref.at[from_right])
+
+        return 0
+
+    lax.fori_loop(1, LINE, advance, 0)
+
+    def drain(step, _):
+        for c in range(2):
+            @pl.when(jnp.logical_and(z - step >= 0, can_right))
+            def _():
+                line_copy(z - step, step, c, 0).wait_send()
+
+            @pl.when(jnp.logical_and(z + step < LINE, can_left))
+            def _():
+                line_copy(z + step, step, c, 1).wait_send()
+
+        for e in range(1, PLANE):
+            plane_copy(step, e).wait()
+        return 0
+
+    lax.fori_loop(0, LINE, drain, 0)
+    swap = swap_matrix()
+    for source in range(PLANE):
+        block = jnp.dot(
+            swap, got[source].reshape(BS, features), preferred_element_type=jnp.float32
+        ).astype(jnp.bfloat16)
+        out_ref[:, source] = block.reshape(8, 16, features)
+
+
+def collect(terms_ref, act_ref, pos_ref, res_ref, stage, got, sums, from_left, from_right, right_sum,
+            left_sum, line_sems, plane_sems, place):
+    z, q = place
+    features = act_ref.shape[1]
+    swap = swap_matrix()
+    for e in range(PLANE):
+        to = (q + e) % PLANE
+        block = jnp.dot(
+            swap, terms_ref[:, to].reshape(BS, features), preferred_element_type=jnp.float32
+        ).astype(jnp.bfloat16)
+        if e == 0:
+            got[q] = block.reshape(LINE, 16, features)
+        else:
+            stage[to] = block.reshape(LINE, 16, features)
+
+    def plane_copy(d, e):
+        to = (q + e) % PLANE
+        return lat_copy(
+            stage.at[to, d], got.at[q, d], plane_sems.at[0, d, e - 1], plane_sems.at[1, d, e - 1], z, to
+        )
+
+    def line_copy(d, far, c, way):
+        land = from_right if way else from_left
+        return lat_copy(
+            sums.at[d, :, half(c, features)],
+            land.at[d, :, half(c, features)],
+            line_sems.at[0, way, far, c],
+            line_sems.at[1, way, far, c],
+            z + 1 - 2 * way,
+            q,
+        )
+
+    def send_out(i, _):
+        far = LINE - 1 - i
+
+        @pl.when(z + far < LINE)
+        def _():
+            for e in range(1, PLANE):
+                plane_copy(z + far, e).start()
+
+        @pl.when(jnp.logical_and(z - far >= 0, far > 0))
+        def _():
+            for e in range(1, PLANE):
+                plane_copy(z - far, e).start()
+
+        return 0
+
+    lax.fori_loop(0, LINE, send_out, 0)
+
+    def partial(d):
+        for e in range(1, PLANE):
+            plane_copy(d, e).wait_recv()
+        hit = slot_matrix(pos_ref[d]).astype(jnp.bfloat16)
+        terms = got[:, d].reshape(BS, features)
+        return lax.dot_general(
+            hit, terms, (((0,), (0,)), ((), ())), preferred_element_type=jnp.float32
+        )
+
+    def advance(i, _):
+        far = LINE - 1 - i
+        right, left = z + far, z - far
+        go_right, go_left = right < LINE, left >= 0
+
+        @pl.when(go_right)
+        def _():
+            right_sum[...] = partial(right)
+
+        @pl.when(go_left)
+        def _():
+            left_sum[...] = partial(left)
+
+        for c in range(2):
+            part = half(c, features)
+
+            @pl.when(go_right)
+            def _():
+                @pl.when(z > 0)
+                def _():
+                    line_copy(right, far + 1, c, 0).wait_recv()
+                    right_sum[:, part] += from_left[right, :, part].astype(jnp.float32)
+
+                sums[right, :, part] = right_sum[:, part].astype(jnp.bfloat16)
+                line_copy(right, far, c, 0).start()
+
+            @pl.when(go_left)
+            def _():
+                @pl.when(z < LINE - 1)
+                def _():
+                    line_copy(left, far + 1, c, 1).wait_recv()
+                    left_sum[:, part] += from_right[left, :, part].astype(jnp.float32)
+
+                sums[left, :, part] = left_sum[:, part].astype(jnp.bfloat16)
+                line_copy(left, far, c, 1).start()
+
+        return 0
+
+    lax.fori_loop(0, LINE - 1, advance, 0)
+    right_sum[...] = partial(z) - act_ref[...].astype(jnp.float32)
+
+    @pl.when(z > 0)
+    def _():
+        for c in range(2):
+            line_copy(z, 1, c, 0).wait_recv()
+        right_sum[...] += from_left[z].astype(jnp.float32)
+
+    @pl.when(z < LINE - 1)
+    def _():
+        for c in range(2):
+            line_copy(z, 1, c, 1).wait_recv()
+        right_sum[...] += from_right[z].astype(jnp.float32)
+
+    res_ref[...] = right_sum[...].astype(jnp.bfloat16)
+
+    def drain(far, _):
+        for c in range(2):
+            @pl.when(jnp.logical_and(z + far < LINE, far > 0))
+            def _():
+                line_copy(z + far, far, c, 0).wait_send()
+
+            @pl.when(jnp.logical_and(z - far >= 0, far > 0))
+            def _():
+                line_copy(z - far, far, c, 1).wait_send()
+
+        for e in range(1, PLANE):
+            plane_copy(far, e).wait_send()
+        return 0
+
+    return drain
+
+
+def spread_kernel(x_ref, out_ref, pos_ref, all_ref, stage, got, line_sems, plane_sems):
+    place = lat_place()
+    greet_lat(place)
+    spread(x_ref, all_ref, pos_ref, stage, got, out_ref, line_sems, plane_sems, place, True)
+
+
+def residual_kernel(terms_ref, act_ref, pos_ref, out_ref, res_ref, stage_t, got_t, sums, from_left,
+                    from_right, right_sum, left_sum, all_ref, stage, got, line_t, plane_t, line_sems,
+                    plane_sems):
+    place = lat_place()
+    greet_lat(place)
+    drain = collect(terms_ref, act_ref, pos_ref, res_ref, stage_t, got_t, sums, from_left, from_right,
+                    right_sum, left_sum, line_t, plane_t, place)
+    spread(res_ref, all_ref, pos_ref, stage, got, out_ref, line_sems, plane_sems, place, False)
+    lax.fori_loop(0, LINE, drain, 0)
+
+
+def slots_buffer(features):
+    return pltpu.VMEM((8, 8, 16, features), jnp.bfloat16)
+
+
+def lat_sems():
+    return [pltpu.SemaphoreType.DMA((2, 2, LINE, 2)), pltpu.SemaphoreType.DMA((2, LINE, PLANE - 1))]
+
+
+def spread_rows(x):
+    rows, features = x.shape
+    return pl.pallas_call(
+        spread_kernel,
+        out_shape=(
+            jax.ShapeDtypeStruct((8, PLANE, 16, features), jnp.bfloat16),
+            jax.ShapeDtypeStruct((LINE, 8, BS), jnp.float32),
+        ),
+        in_specs=vmem(1),
+        out_specs=tuple(vmem(2)),
+        scratch_shapes=[
+            pltpu.VMEM((LINE, rows, features), jnp.bfloat16),
+            slots_buffer(features),
+            slots_buffer(features),
+        ]
+        + lat_sems(),
+        compiler_params=pltpu.CompilerParams(collective_id=2, has_side_effects=True),
+        name="spread_rows",
+    )(x)
+
+
+def spread_residual(terms, activations, pos):
+    rows, features = activations.shape
+    row_blocks = pltpu.VMEM((LINE, rows, features), jnp.bfloat16)
+    return pl.pallas_call(
+        residual_kernel,
+        out_shape=jax.ShapeDtypeStruct((8, PLANE, 16, features), jnp.bfloat16),
+        in_specs=vmem(3),
+        out_specs=vmem(1)[0],
+        scratch_shapes=[
+            pltpu.VMEM((rows, features), jnp.bfloat16),
+            slots_buffer(features),
+            slots_buffer(features),
+            row_blocks,
+            row_blocks,
+            row_blocks,
+            pltpu.VMEM((rows, features), jnp.float32),
+            pltpu.VMEM((rows, features), jnp.float32),
+            row_blocks,
+            slots_buffer(features),
+            slots_buffer(features),
+        ]
+        + lat_sems()
+        + lat_sems(),
+        compiler_params=pltpu.CompilerParams(collective_id=3, has_side_effects=True),
+        name="spread_residual",
+    )(terms, activations, pos)
 
 
 def body(activations, block_ids, alive_tallies, encoder, encoder_bias, decoder):
@@ -208,7 +571,6 @@
     slots = block_ids.shape[1]
     lat = lax.axis_size("lat")
     wid = lax.axis_index("wid")
-    positions = lat * 16
     f32 = jnp.float32
 
     flat = block_ids.reshape(rows * slots)
@@ -216,17 +578,12 @@
     earlier = (flat[:, None] == flat[None, :]) & (order[None, :] < order[:, None])
     rank = jnp.sum(earlier.astype(jnp.int32), axis=1).reshape(rows, slots)
     alive = jnp.arange(slots, dtype=jnp.int32)[None, :] < alive_tallies[:, None]
-    position = jnp.where(alive, block_ids * 2 + rank, -1)
-    spots = jnp.arange(positions, dtype=jnp.int32)[:, None]
-    place = spots == position[:, 0][None, :]
-    for j in range(1, slots):
-        place = place | (spots == position[:, j][None, :])
-    filled = jnp.any(place, axis=1, keepdims=True)
-    place = place.astype(jnp.bfloat16)
-
-    outgoing = jnp.dot(place, activations, preferred_element_type=f32)
-    outgoing = jnp.where(filled, outgoing, FILLER).astype(jnp.bfloat16)
-    incoming = to_owner(outgoing, lat)
+    position = block_ids * 2 + rank
+    high = jnp.where(alive, position >> 3, 255)
+    codes_of_rows = jnp.concatenate([high, position & 7], axis=1).T.astype(jnp.bfloat16)
+    extra = jnp.pad(codes_of_rows, ((0, 8), (0, features - rows)))
+    incoming, pos = spread_rows(jnp.concatenate([activations, extra], axis=0))
+    incoming = incoming.reshape(8, lat * 2, features)
     live = (incoming[:, :, 0] < 1.5).astype(f32)
     own_live = jnp.broadcast_to(
         lax.dynamic_index_in_dim(live, wid, 0, keepdims=False)[:, None], (lat * 2, BS)
@@ -247,11 +604,8 @@
     unit = (decoder_wide.reshape(8, BS, features) / row_norm).astype(jnp.bfloat16)
 
     terms = jnp.einsum("jkr,jrs->jks", codes, unit, preferred_element_type=f32).astype(jnp.bfloat16)
-    returned = to_row(terms, lat)
-    recon = lax.dot_general(place, returned, (((0,), (0,)), ((), ())), preferred_element_type=f32)
-    residual = (recon - activations.astype(f32)).astype(jnp.bfloat16)
-    resid_send = jnp.dot(place, residual, preferred_element_type=f32).astype(jnp.bfloat16)
-    resid_in = to_owner(resid_send, lat)
+    resid_in = spread_residual(terms.reshape(8, PLANE, 16, features), activations, pos)
+    resid_in = resid_in.reshape(8, lat * 2, features)
 
     partial_dcode = jnp.einsum(
         "zea,zxa->zex", resid_in, unit, preferred_element_type=f32

time: 293 us -> 209 us (0.71); the launches traced: 288 us -> 208 us
  Pallas kernels: 61 us -> 187 us
  blocking collectives: 123 us -> 0 us
  waiting for transfers between devices: 49.4 us -> 0 us
  starting transfers between devices: 17.2 us -> 0 us
  local copies, waits for them, and re-layouts: 19.1 us -> 7.64 us
  matrix products: 13.6 us -> 8.33 us
    all_to_all x2 -> x0, blocking collectives: 123 us -> none  [the longest x1 63.6 us: to_row(): x = lax.all_to_all(x, 'lat', split_axis=0, concat_axis=0, tiled=True)]
    pallas_call x0 -> x2, Pallas kernels: none -> 123 us  [the longest x1 77.4 us: spread_residual(): pl.pallas_call(residual_kernel, out_shape=jax.ShapeDtypeStruct((8, PLANE,...]
    all_to_all x1 -> x0, waiting for transfers between devices: 49.4 us -> none  [to_owner(): lax.all_to_all(x.reshape(lat, 16, features), 'lat', split_axis=0, concat_...]
    all_to_all x1 -> x0, starting transfers between devices: 17.2 us -> none  [to_owner(): lax.all_to_all(x.reshape(lat, 16, features), 'lat', split_axis=0, concat_...]
    reshape x9 -> x0, local copies, waits for them, and re-layouts: 13.2 us -> none  [the longest x6 9 us: to_owner(): x.reshape(lat, 8, 2, features).transpose(1, 0, 2, 3)]
    dot_general x2 -> x0, matrix products: 5.35 us -> none  [the longest x1 3.04 us: body(): jnp.dot(place, residual, preferred_element_type=f32).astype(jnp.bfloat16)]
  transfers between devices with their start and end apart: 1 -> 0, of which waited for: 1 -> 0; matrix products, arithmetic and copies ran while one was open for 1% -> 0% of each run, Pallas kernels for 0% -> 0%
where the time goes in v2:
time: 209 us; the launch traced here: 208 us
  Pallas kernels  187 us (89%)
  matrix products  8.33 us (4%)
  local copies, waits for them, and re-layouts  7.64 us (4%)
  other arithmetic  4.43 us (2%)
    pallas_call x1, Pallas kernels, spread_residual(): pl.pallas_call(residual_kernel, out_shape=jax.ShapeDtypeStruct((8, PLANE,...  77.4 us
    pallas_call x1, Pallas kernels, spread_rows(): pl.pallas_call(spread_kernel, out_shape=(jax.ShapeDtypeStruct((8, PLANE,...  45.4 us
    pallas_call x1, Pallas kernels, forward_sums(): pl.pallas_call(forward_kernel, out_shape=(jax.ShapeDtypeStruct((2, 4, slo...  35.3 us
    pallas_call x1, Pallas kernels, backward_sums(): pl.pallas_call(backward_kernel, out_shape=(jax.ShapeDtypeStruct((2, 4, sl...  29 us

profile of v2, /device:TPU:1, one launch (start us, length us, event | category | flops | bytes accessed | tf_op | source)
XLA Modules:
  0.0 208.1 jit_solution(4245055320652593050)
XLA Ops:
  0.6 0.9 copy.21
  1.5 0.1 eq.15
  1.6 0.3 convert_reduce_fusion
  1.9 0.1 reshape.62
  2.1 0.7 select_convert_fusion
  2.8 1.6 fusion.4.x_ref
  4.4 45.4 %spread_rows.1 = (bf16[8,8,16,512]{3,2,1,0:T(8,128)(2,1)}, f32[8,8,128]{2,1,0:T(8,128)}) custom-call(bf16[144,512]{1,0:T(8,128)(2,1)} %fusion.4.x_ref), custom_call_target="tpu_custom_call" | custom-call | tf_op jit(solution)/shard_map/spread_rows/pallas_call | solution.py:522
  49.7 1.0 slice.12
  50.8 0.7 broadcast_in_dim.10.live_ref
  51.6 1.3 constant_dynamic-slice_fusion.1.bias_ref
  52.8 2.5 %convolution_convert_fusion.3 = bf16[8,128,128]{2,1,0:T(8,128)(2,1)} fusion(bf16[8,128,512]{2,1,0:T(8,128)(2,1)} %bitcast.44, bf16[512,1024]{1,0:T(8,128)(2,1)S(1)} %copy-done), kind=kOutput, calls=%fused_computation.6 | convolution fusion | flops 134348800 | bytes 2359296 | tf_op jit(solution)/shard_map/aec,caw->aew/dot_general | solution.py:595
  55.3 0.9 multiply_reduce_fusion
  56.2 35.3 %forward_sums.1 = (bf16[2,4,128,128]{3,2,1,0:T(8,128)(2,1)}, f32[128,128]{1,0:T(8,128)}, bf16[128,128]{1,0:T(8,128)(2,1)}, f32[8,128]{1,0:T(8,128)}) custom-call(bf16[2,4,128,128]{3,2,1,0:T(8,128)(2,1)} %bitcast.50, f32[8,128]{1,0:T(8,128)} %bitcast.51, f32[1,128]{1,0:T(1,128)} %constant_dynamic-slice_fusion.1.bias_ref, f32[128,128]{1,0:T(8,128)} %broadcast_in_dim.10.live_ref), custom_call_target="tpu_custom_call" | custom-call | tf_op jit(solution)/shard_map/forward_sums/pallas_call | solution.py:157
  91.4 0.7 add_sqrt_fusion
  92.1 0.3 divide_convert_fusion.1
  92.4 0.6 copy-done.4
  93.1 1.4 convolution_convert_fusion.1
  94.5 77.4 %spread_residual.1 = bf16[8,8,16,512]{3,2,1,0:T(8,128)(2,1)} custom-call(bf16[8,8,16,512]{3,2,1,0:T(8,128)(2,1)} %bitcast.41, bf16[128,512]{1,0:T(8,128)(2,1)} %act_ref.1, f32[8,8,128]{2,1,0:T(8,128)} %get-tuple-element.14.pos_ref), custom_call_target="tpu_custom_call" | custom-call | tf_op jit(solution)/shard_map/spread_residual/pallas_call | solution.py:544
  171.9 2.4 %convolution_convert_fusion.2 = bf16[8,128,128]{2,1,0:T(8,128)(2,1)} fusion(bf16[8,128,512]{2,1,0:T(8,128)(2,1)} %bitcast.39, bf16[8,128,512]{2,1,0:T(8,128)(2,1)S(1)} %divide_convert_fusion.1), kind=kOutput, calls=%fused_computation.5 | convolution fusion | flops 134348800 | bytes 2359296 | tf_op jit(solution)/shard_map/zea,zxa->zex/dot_general | solution.py:610
  174.3 29.0 %backward_sums.1 = (bf16[2,4,128,128]{3,2,1,0:T(8,128)(2,1)}, f32[2,4,8,128]{3,2,1,0:T(8,128)}) custom-call(bf16[2,4,128,128]{3,2,1,0:T(8,128)(2,1)} %bitcast.46, f32[128,128]{1,0:T(8,128)} %get-tuple-element.15.pre_ref, bf16[128,128]{1,0:T(8,128)(2,1)} %get-tuple-element.16.own_ref, f32[128,128]{1,0:T(8,128)} %broadcast_in_dim.10.live_ref), custom_call_target="tpu_custom_call" | custom-call | tf_op jit(solution)/shard_map/backward_sums/pallas_call | solution.py:181
  203.3 1.4 fusion.6
  204.8 1.5 divide_convert_fusion
  206.3 0.5 convolution_convert_fusion
  206.8 1.3 copy.27
  (16 shorter events, 0.2 us)
Async XLA Ops:
  0.6 52.2 %copy-start = (bf16[512,1024]{1,0:T(8,128)(2,1)S(1)}, bf16[512,1024]{1,0:T(8,128)(2,1)}, u32[]{:S(2)}) copy-start(bf16[512,1024]{1,0:T(8,128)(2,1)} %param.9) | copy-start | bytes 3145732
  52.8 2.5 %copy-start.1 = (bf16[1024,512]{1,0:T(8,128)(2,1)S(1)}, bf16[1024,512]{1,0:T(8,128)(2,1)}, u32[]{:S(2)}) copy-start(bf16[1024,512]{1,0:T(8,128)(2,1)} %param.11) | copy-start | bytes 3145732
  92.1 1.0 copy-start.4
  171.9 32.9 %copy-start.2 = (bf16[8,8,16,512]{3,2,1,0:T(8,128)(2,1)S(1)}, bf16[8,8,16,512]{3,2,1,0:T(8,128)(2,1)}, u32[]{:S(2)}) copy-start(bf16[8,8,16,512]{3,2,1,0:T(8,128)(2,1)} %spread_residual.1) | copy-start | bytes 3145732
  204.8 1.6 copy-start.3
  204.8 1.6 copy-start.5

commit v3 on v2

--- a/solution.py
+++ b/solution.py
@@ -1,5 +1,3 @@
-import functools
-
 import jax
 import jax.numpy as jnp
 from jax import lax
@@ -32,13 +30,6 @@
     partner = (1 - hi) * 4 + y
     peers = [hi * 4 + (y + d) % 4 for d in (1, 2, 3)]
     return hi, y, partner, peers
-
-
-def greet(others):
-    barrier = pltpu.get_barrier_semaphore()
-    for other in others:
-        pl.semaphore_signal(barrier, inc=1, device_id={"wid": other}, device_id_type=MESH)
-    pl.semaphore_wait(barrier, len(others))
 
 
 def send(src, dst, send_sem, recv_sem, to):
@@ -54,12 +45,14 @@
     return copy
 
 
-def scatter_sums(part_ref, got_y, mine, got_z, sems, place):
+def scatter_sums(part_ref, got_y, mine, got_z, sems, place, meanwhile=None):
     hi, y, partner, peers = place
     copies = [
         send(part_ref.at[:, (y + d) % 4], got_y.at[d - 1], sems.at[0, d - 1], sems.at[1, d - 1], peers[d - 1])
         for d in (1, 2, 3)
     ]
+    if meanwhile is not None:
+        meanwhile()
     for copy in copies:
         copy.wait()
 
@@ -96,50 +89,6 @@
     ]
 
 
-def forward_kernel(part_ref, sq_ref, bias_ref, live_ref, codes_ref, pre_ref, own_ref, row_ref,
-                   got_y, mine, got_z, sq_y, sq_mine, sq_z, sems):
-    place = wid_place()
-    hi, y, partner, peers = place
-    greet([partner] + peers)
-    sq_copies = [
-        send(sq_ref, sq_y.at[d - 1], sems.at[0, 10 + d], sems.at[1, 10 + d], peers[d - 1]) for d in (1, 2, 3)
-    ]
-    for copy in sq_copies:
-        copy.wait()
-    sq_mine[...] = sq_ref[...] + sq_y[0] + sq_y[1] + sq_y[2]
-    sq_far = send(sq_mine, sq_z, sems.at[0, 14], sems.at[1, 14], partner)
-    preact = scatter_sums(part_ref, got_y, mine, got_z, sems, place) + bias_ref[...]
-    pre_ref[...] = preact
-    codes = (gelu(preact) * live_ref[...]).astype(jnp.bfloat16)
-    own_ref[...] = codes
-    codes_ref[hi, y] = codes
-    far, near = gather_start(codes_ref, sems, 4, place)
-    sq_far.wait()
-    row_ref[...] = sq_mine[...] + sq_z[...]
-    late = gather_pass(codes_ref, sems, 4, far, place)
-    for copy in near + late:
-        copy.wait()
-
-
-def backward_kernel(part_ref, pre_ref, own_ref, live_ref, dpre_ref, small_ref, got_y, mine, got_z, sems):
-    place = wid_place()
-    hi, y, partner, peers = place
-    greet([partner] + peers)
-    dcode = scatter_sums(part_ref, got_y, mine, got_z, sems, place)
-    dpre = dcode * gelu_slope(pre_ref[...]) * live_ref[...]
-    dpre_ref[hi, y] = dpre.astype(jnp.bfloat16)
-    far, near = gather_start(dpre_ref, sems, 4, place)
-    along = jnp.sum(own_ref[...].astype(jnp.float32) * dcode, axis=0, keepdims=True)
-    bias_grad = jnp.sum(dpre, axis=0, keepdims=True)
-    row = lax.broadcasted_iota(jnp.int32, (8, BS), 0)
-    small_ref[hi, y] = jnp.where(row == 0, along, bias_grad)
-    small_far, small_near = gather_start(small_ref, sems, 11, place)
-    late = gather_pass(dpre_ref, sems, 4, far, place)
-    small_late = gather_pass(small_ref, sems, 11, small_far, place)
-    for copy in near + late + small_near + small_late:
-        copy.wait()
-
-
 def vmem(n):
     return [pl.BlockSpec(memory_space=pltpu.VMEM)] * n
 
@@ -152,78 +101,41 @@
     ]
 
 
-def forward_sums(part, sq, bias, live):
-    slots = part.shape[2]
-    return pl.pallas_call(
-        forward_kernel,
-        out_shape=(
-            jax.ShapeDtypeStruct((2, 4, slots, BS), jnp.bfloat16),
-            jax.ShapeDtypeStruct((slots, BS), jnp.float32),
-            jax.ShapeDtypeStruct((slots, BS), jnp.bfloat16),
-            jax.ShapeDtypeStruct((8, BS), jnp.float32),
-        ),
-        in_specs=vmem(4),
-        out_specs=tuple(vmem(4)),
-        scratch_shapes=sum_scratch(slots)
-        + [
-            pltpu.VMEM((3, 8, BS), jnp.float32),
-            pltpu.VMEM((8, BS), jnp.float32),
-            pltpu.VMEM((8, BS), jnp.float32),
-            pltpu.SemaphoreType.DMA((2, 15)),
-        ],
-        compiler_params=pltpu.CompilerParams(collective_id=0, has_side_effects=True),
-        name="forward_sums",
-    )(part, sq, bias, live)
-
-
-def backward_sums(part, pre, own, live):
-    slots = part.shape[2]
-    return pl.pallas_call(
-        backward_kernel,
-        out_shape=(
-            jax.ShapeDtypeStruct((2, 4, slots, BS), jnp.bfloat16),
-            jax.ShapeDtypeStruct((2, 4, 8, BS), jnp.float32),
-        ),
-        in_specs=vmem(4),
-        out_specs=tuple(vmem(2)),
-        scratch_shapes=sum_scratch(slots) + [pltpu.SemaphoreType.DMA((2, 18))],
-        compiler_params=pltpu.CompilerParams(collective_id=1, has_side_effects=True),
-        name="backward_sums",
-    )(part, pre, own, live)
-
-
 def lat_place():
     me = lax.axis_index("lat")
     return me // PLANE, me % PLANE
 
 
-def greet_lat(place):
+def greet(place, wid):
     z, q = place
+    _, _, partner, peers = wid
     barrier = pltpu.get_barrier_semaphore()
 
-    def signal(other):
-        pl.semaphore_signal(barrier, inc=1, device_id={"lat": other}, device_id_type=MESH)
-
+    def signal(**other):
+        pl.semaphore_signal(barrier, inc=1, device_id=other, device_id_type=MESH)
+
+    for other in [partner] + peers:
+        signal(wid=other)
     for e in range(1, PLANE):
-        signal(z * PLANE + (q + e) % PLANE)
+        signal(lat=z * PLANE + (q + e) % PLANE)
 
     @pl.when(z > 0)
     def _():
-        signal((z - 1) * PLANE + q)
+        signal(lat=(z - 1) * PLANE + q)
 
     @pl.when(z < LINE - 1)
     def _():
-        signal((z + 1) * PLANE + q)
+        signal(lat=(z + 1) * PLANE + q)
 
     inner = jnp.logical_and(z > 0, z < LINE - 1)
 
     @pl.when(inner)
     def _():
-        pl.semaphore_wait(barrier, PLANE + 1)
+        pl.semaphore_wait(barrier, PLANE + 5)
 
     @pl.when(jnp.logical_not(inner))
     def _():
-        pl.semaphore_wait(barrier, PLANE)
+        pl.semaphore_wait(barrier, PLANE + 4)
 
 
 def lat_copy(src, dst, send_sem, recv_sem, z, q):
@@ -256,16 +168,17 @@
     return jnp.where(source == col, 1.0, 0.0).astype(jnp.bfloat16)
 
 
-def spread(x_ref, all_ref, pos_ref, stage, got, out_ref, line_sems, plane_sems, place, first):
+def spread(x_ref, all_ref, pos_ref, stage, got, out_ref, line_sems, plane_sems, place, first, meanwhile=None):
     z, q = place
     rows = BS
     features = x_ref.shape[1]
 
     def line_copy(b, step, c, way, src=None):
         src = all_ref.at[b] if src is None else src
+        height = pl.ds(0, rows if c else x_ref.shape[0])
         return lat_copy(
-            src.at[:, half(c, features)],
-            all_ref.at[b, :, half(c, features)],
+            src.at[height, half(c, features)],
+            all_ref.at[b, height, half(c, features)],
             line_sems.at[0, way, step, c],
             line_sems.at[1, way, step, c],
             z + 1 - 2 * way,
@@ -307,6 +220,8 @@
             line_copy(z, 0, c, 1, x_ref).start()
 
     select(z, x_ref)
+    if meanwhile is not None:
+        meanwhile()
 
     def advance(step, _):
         from_left, from_right = z - step, z + step
@@ -492,21 +407,99 @@
     return drain
 
 
-def spread_kernel(x_ref, out_ref, pos_ref, all_ref, stage, got, line_sems, plane_sems):
+def column(row):
+    r = lax.broadcasted_iota(jnp.int32, (BS, BS), 0)
+    col = lax.broadcasted_iota(jnp.int32, (BS, BS), 1)
+    return jnp.sum(jnp.where(r == col, row, 0.0), axis=1, keepdims=True)
+
+
+def step_kernel(x_ref, sq_ref, bias_ref, enc_ref, dec_ref,
+                in_ref, resid_ref, codes_ref, dpre_ref, unit_ref, row_ref, small_ref,
+                all_a, stage_a, got_a, line_a, plane_a,
+                sq_y, sq_mine, sq_z,
+                part_b, got_yb, mine_b, got_zb, pre_ref, own_ref, sems_b,
+                terms_ref, res_ref, stage_c, got_c, sums, from_left, from_right, right_sum, left_sum,
+                line_c, plane_c,
+                all_d, stage_d, got_d, line_d, plane_d,
+                part_e, got_ye, mine_e, got_ze, sems_e, pos_ref):
     place = lat_place()
-    greet_lat(place)
-    spread(x_ref, all_ref, pos_ref, stage, got, out_ref, line_sems, plane_sems, place, True)
-
-
-def residual_kernel(terms_ref, act_ref, pos_ref, out_ref, res_ref, stage_t, got_t, sums, from_left,
-                    from_right, right_sum, left_sum, all_ref, stage, got, line_t, plane_t, line_sems,
-                    plane_sems):
-    place = lat_place()
-    greet_lat(place)
-    drain = collect(terms_ref, act_ref, pos_ref, res_ref, stage_t, got_t, sums, from_left, from_right,
-                    right_sum, left_sum, line_t, plane_t, place)
-    spread(res_ref, all_ref, pos_ref, stage, got, out_ref, line_sems, plane_sems, place, False)
+    wid = wid_place()
+    hi, y, partner, peers = wid
+    rows = BS
+    features = x_ref.shape[1]
+    f32, bf16 = jnp.float32, jnp.bfloat16
+    greet(place, wid)
+
+    sq_copies = [
+        send(sq_ref, sq_y.at[d - 1], sems_b.at[0, 10 + d], sems_b.at[1, 10 + d], peers[d - 1])
+        for d in (1, 2, 3)
+    ]
+    sq_far = pltpu.make_async_remote_copy(
+        src_ref=sq_mine, dst_ref=sq_z, send_sem=sems_b.at[0, 14], recv_sem=sems_b.at[1, 14],
+        device_id={"wid": partner}, device_id_type=MESH,
+    )
+
+    def sum_squares():
+        for copy in sq_copies:
+            copy.wait()
+        sq_mine[...] = sq_ref[...] + sq_y[0] + sq_y[1] + sq_y[2]
+        sq_far.start()
+
+    spread(x_ref, all_a, pos_ref, stage_a, got_a, in_ref, line_a, plane_a, place, True, sum_squares)
+
+    for k in range(8):
+        part_b[k // 4, k % 4] = jnp.dot(
+            in_ref[k].reshape(BS, features), enc_ref[:, k * BS : (k + 1) * BS], preferred_element_type=f32
+        ).astype(bf16)
+
+    def normalize():
+        sq_far.wait()
+        row_ref[...] = jnp.sqrt(sq_mine[...] + sq_z[...] + EPS)
+        for k in range(8):
+            norm = column(row_ref[k : k + 1, :])
+            unit_ref[k] = (dec_ref[k].astype(f32) / norm).astype(bf16)
+
+    mine = hi * 4 + y
+    preact = scatter_sums(part_b, got_yb, mine_b, got_zb, sems_b, wid, normalize) + bias_ref[mine]
+    pre_ref[...] = preact
+    live = in_ref[mine].reshape(BS, features)[:, 0:1].astype(f32) < 1.5
+    codes = jnp.where(live, gelu(preact), 0.0).astype(bf16)
+    own_ref[...] = codes
+    codes_ref[hi, y] = codes
+    far, near = gather_start(codes_ref, sems_b, 4, wid)
+    late = gather_pass(codes_ref, sems_b, 4, far, wid)
+    for copy in near + late:
+        copy.wait()
+
+    for k in range(8):
+        terms_ref[k] = (
+            jnp.dot(codes_ref[k // 4, k % 4], unit_ref[k], preferred_element_type=f32)
+            .astype(bf16)
+            .reshape(PLANE, 16, features)
+        )
+    drain = collect(terms_ref, x_ref.at[0:rows, :], pos_ref, res_ref, stage_c, got_c, sums, from_left,
+                    from_right, right_sum, left_sum, line_c, plane_c, place)
+    spread(res_ref, all_d, pos_ref, stage_d, got_d, resid_ref, line_d, plane_d, place, False)
+
+    for k in range(8):
+        part_e[k // 4, k % 4] = lax.dot_general(
+            resid_ref[k].reshape(BS, features), unit_ref[k], (((1,), (1,)), ((), ())),
+            preferred_element_type=f32,
+        ).astype(bf16)
+    dcode = scatter_sums(part_e, got_ye, mine_e, got_ze, sems_e, wid)
+    dpre = jnp.where(live, dcode * gelu_slope(pre_ref[...]), 0.0)
+    dpre_ref[hi, y] = dpre.astype(bf16)
+    far, near = gather_start(dpre_ref, sems_e, 4, wid)
+    along = jnp.sum(own_ref[...].astype(f32) * dcode, axis=0, keepdims=True)
+    bias_grad = jnp.sum(dpre, axis=0, keepdims=True)
+    row = lax.broadcasted_iota(jnp.int32, (8, BS), 0)
+    small_ref[hi, y] = jnp.where(row == 0, along, bias_grad)
+    small_far, small_near = gather_start(small_ref, sems_e, 11, wid)
     lax.fori_loop(0, LINE, drain, 0)
+    late = gather_pass(dpre_ref, sems_e, 4, far, wid)
+    small_late = gather_pass(small_ref, sems_e, 11, small_far, wid)
+    for copy in near + late + small_near + small_late:
+        copy.wait()
 
 
 def slots_buffer(features):
@@ -517,60 +510,51 @@
     return [pltpu.SemaphoreType.DMA((2, 2, LINE, 2)), pltpu.SemaphoreType.DMA((2, LINE, PLANE - 1))]
 
 
-def spread_rows(x):
-    rows, features = x.shape
+def run_step(x, sq, bias, encoder, decoder):
+    rows, features = BS, x.shape[1]
+    f32, bf16 = jnp.float32, jnp.bfloat16
+    slots = 2 * LINE * PLANE
+    row_blocks = pltpu.VMEM((LINE, rows, features), bf16)
+    slot = slots_buffer(features)
+    wid_part = pltpu.VMEM((2, 4, slots, BS), bf16)
+    sq_block = pltpu.VMEM((8, BS), f32)
+    row_total = pltpu.VMEM((rows, features), f32)
     return pl.pallas_call(
-        spread_kernel,
+        step_kernel,
         out_shape=(
-            jax.ShapeDtypeStruct((8, PLANE, 16, features), jnp.bfloat16),
-            jax.ShapeDtypeStruct((LINE, 8, BS), jnp.float32),
+            jax.ShapeDtypeStruct((8, PLANE, 16, features), bf16),
+            jax.ShapeDtypeStruct((8, PLANE, 16, features), bf16),
+            jax.ShapeDtypeStruct((2, 4, slots, BS), bf16),
+            jax.ShapeDtypeStruct((2, 4, slots, BS), bf16),
+            jax.ShapeDtypeStruct((8, BS, features), bf16),
+            jax.ShapeDtypeStruct((8, BS), f32),
+            jax.ShapeDtypeStruct((2, 4, 8, BS), f32),
         ),
-        in_specs=vmem(1),
-        out_specs=tuple(vmem(2)),
-        scratch_shapes=[
-            pltpu.VMEM((LINE, rows, features), jnp.bfloat16),
-            slots_buffer(features),
-            slots_buffer(features),
-        ]
-        + lat_sems(),
-        compiler_params=pltpu.CompilerParams(collective_id=2, has_side_effects=True),
-        name="spread_rows",
-    )(x)
-
-
-def spread_residual(terms, activations, pos):
-    rows, features = activations.shape
-    row_blocks = pltpu.VMEM((LINE, rows, features), jnp.bfloat16)
-    return pl.pallas_call(
-        residual_kernel,
-        out_shape=jax.ShapeDtypeStruct((8, PLANE, 16, features), jnp.bfloat16),
-        in_specs=vmem(3),
-        out_specs=vmem(1)[0],
-        scratch_shapes=[
-            pltpu.VMEM((rows, features), jnp.bfloat16),
-            slots_buffer(features),
-            slots_buffer(features),
-            row_blocks,
-            row_blocks,
-            row_blocks,
-            pltpu.VMEM((rows, features), jnp.float32),
-            pltpu.VMEM((rows, features), jnp.float32),
-            row_blocks,
-            slots_buffer(features),
-            slots_buffer(features),
-        ]
+        in_specs=vmem(5),
+        out_specs=tuple(vmem(7)),
+        scratch_shapes=[pltpu.VMEM((LINE, x.shape[0], features), bf16), slot, slot]
         + lat_sems()
-        + lat_sems(),
-        compiler_params=pltpu.CompilerParams(collective_id=3, has_side_effects=True),
-        name="spread_residual",
-    )(terms, activations, pos)
+        + [pltpu.VMEM((3, 8, BS), f32), sq_block, sq_block]
+        + [wid_part]
+        + sum_scratch(slots)
+        + [pltpu.VMEM((slots, BS), f32), pltpu.VMEM((slots, BS), bf16), pltpu.SemaphoreType.DMA((2, 15))]
+        + [slot, pltpu.VMEM((rows, features), bf16), slot, slot]
+        + [row_blocks, row_blocks, row_blocks, row_total, row_total]
+        + lat_sems()
+        + [row_blocks, slot, slot]
+        + lat_sems()
+        + [wid_part]
+        + sum_scratch(slots)
+        + [pltpu.SemaphoreType.DMA((2, 18)), pltpu.VMEM((LINE, 8, BS), f32)],
+        compiler_params=pltpu.CompilerParams(collective_id=0, has_side_effects=True),
+        name="step",
+    )(x, sq, bias, encoder, decoder)
 
 
 def body(activations, block_ids, alive_tallies, encoder, encoder_bias, decoder):
     rows, features = activations.shape
     slots = block_ids.shape[1]
     lat = lax.axis_size("lat")
-    wid = lax.axis_index("wid")
     f32 = jnp.float32
 
     flat = block_ids.reshape(rows * slots)
@@ -582,39 +566,20 @@
     high = jnp.where(alive, position >> 3, 255)
     codes_of_rows = jnp.concatenate([high, position & 7], axis=1).T.astype(jnp.bfloat16)
     extra = jnp.pad(codes_of_rows, ((0, 8), (0, features - rows)))
-    incoming, pos = spread_rows(jnp.concatenate([activations, extra], axis=0))
+    local_sq = jnp.sum(jnp.square(decoder.astype(f32)), axis=1).reshape(8, BS)
+    incoming, resid_in, codes, dpre, unit, row_norm, small = run_step(
+        jnp.concatenate([activations, extra], axis=0),
+        local_sq,
+        encoder_bias.reshape(8, 1, BS),
+        encoder,
+        decoder.reshape(8, BS, features),
+    )
     incoming = incoming.reshape(8, lat * 2, features)
-    live = (incoming[:, :, 0] < 1.5).astype(f32)
-    own_live = jnp.broadcast_to(
-        lax.dynamic_index_in_dim(live, wid, 0, keepdims=False)[:, None], (lat * 2, BS)
-    )
-
-    decoder_wide = decoder.astype(f32)
-    local_sq = jnp.sum(jnp.square(decoder_wide), axis=1).reshape(8, BS)
-    encoder_blocks = encoder.reshape(features, 8, BS)
-    partial_pre = jnp.einsum(
-        "aec,caw->aew", incoming, encoder_blocks, preferred_element_type=f32
-    ).astype(jnp.bfloat16)
-    own_bias = lax.dynamic_index_in_dim(encoder_bias.reshape(8, BS), wid, 0, keepdims=True)
-    codes, own_pre, own_codes, row_sq = forward_sums(
-        partial_pre.reshape(2, 4, lat * 2, BS), local_sq, own_bias, own_live
-    )
+    resid_in = resid_in.reshape(8, lat * 2, features)
     codes = codes.reshape(8, lat * 2, BS)
-    row_norm = jnp.sqrt(row_sq + EPS)[:, :, None]
-    unit = (decoder_wide.reshape(8, BS, features) / row_norm).astype(jnp.bfloat16)
-
-    terms = jnp.einsum("jkr,jrs->jks", codes, unit, preferred_element_type=f32).astype(jnp.bfloat16)
-    resid_in = spread_residual(terms.reshape(8, PLANE, 16, features), activations, pos)
-    resid_in = resid_in.reshape(8, lat * 2, features)
-
-    partial_dcode = jnp.einsum(
-        "zea,zxa->zex", resid_in, unit, preferred_element_type=f32
-    ).astype(jnp.bfloat16)
-    dpre, small = backward_sums(
-        partial_dcode.reshape(2, 4, lat * 2, BS), own_pre, own_codes, own_live
-    )
     dpre = dpre.reshape(8, lat * 2, BS)
     small = small.reshape(8, 8, BS)
+    row_norm = row_norm[:, :, None]
     raw = jnp.einsum("ekc,ekv->ecv", codes, resid_in, preferred_element_type=f32)
     along = small[:, 0, :, None]
     bias_grad = small[:, 1].reshape(8 * BS)

time: 209 us -> 183 us (0.88)
  Pallas kernels: 187 us -> 169 us
  matrix products: 8.33 us -> 3.76 us
  local copies, waits for them, and re-layouts: 7.64 us -> 3.82 us
    pallas_call x4 -> x1, Pallas kernels: 187 us -> 169 us  [run_step(): pl.pallas_call(step_kernel, out_shape=(jax.ShapeDtypeStruct((8, PLANE, 16...]
    dot_general x3 -> x0, matrix products: 6.31 us -> none  [the longest x1 2.47 us: body(): jnp.einsum('aec,caw->aew', incoming, encoder_blocks, preferred_element_ty...]
where the time goes in v3:
time: 183 us; the launch traced here: 182 us
  Pallas kernels  169 us (92%)
  other arithmetic  4.66 us (3%)
  local copies, waits for them, and re-layouts  3.82 us (2%)
  matrix products  3.76 us (2%)
    pallas_call x1, Pallas kernels, run_step(): pl.pallas_call(step_kernel, out_shape=(jax.ShapeDtypeStruct((8, PLANE, 16...  169 us

profile of v3, /device:TPU:1, one launch (start us, length us, event | category | flops | bytes accessed | tf_op | source)
XLA Modules:
  0.0 181.9 jit_solution(9899265161930063273)
XLA Ops:
  0.6 0.8 copy.17
  1.4 0.1 eq.15
  1.5 0.3 convert_reduce_fusion
  1.8 0.1 reshape.43
  1.9 0.1 copy.18
  2.0 0.7 select_convert_fusion
  2.7 1.6 fusion.2.x_ref
  4.3 2.1 %multiply_reduce_fusion = f32[1024]{0:T(1024)} fusion(bf16[1024,512]{1,0:T(8,128)(2,1)} %param.11), kind=kLoop, calls=%fused_computation.1 | loop fusion | flops 1571840 | bytes 1052672 | tf_op jit(solution)/shard_map/reduce_sum | solution.py:569
  6.4 169.0 %step.1 = (bf16[8,8,16,512]{3,2,1,0:T(8,128)(2,1)}, bf16[8,8,16,512]{3,2,1,0:T(8,128)(2,1)}, bf16[2,4,128,128]{3,2,1,0:T(8,128)(2,1)}, bf16[2,4,128,128]{3,2,1,0...) custom-call(bf16[144,512]{1,0:T(8,128)(2,1)} %fusion.2.x_ref, ...), custom_call_target="tpu_custom_call" | custom-call | tf_op jit(solution)/shard_map/step/pallas_call | solution.py:522
  175.3 1.4 fusion.3
  176.8 0.0 copy-start
  176.8 0.0 copy-start.1
  176.8 3.3 %divide_convert_fusion = bf16[8,128,512]{2,1,0:T(8,128)(2,1)} fusion(bf16[8,128,512]{2,1,0:T(8,128)(2,1)} %get-tuple-element.15, bf16[8,128,128]{2,1,0:T(8,128)(2,1)} %bitcast.30, bf16[8,128,512]{2,1,0:T(8,128)(2,1)} %bitcast.29, f32[8,128]{1,0:T(8,128)} %get-tuple-element.16, f32[8,128]{1,0:T(8,128)S(1)} %bitcast.27), kind=kOutput, calls=%fused_computation | convolution fusion | flops 136839168 | bytes 3416064 | tf_op jit(solution)/shard_map/ekc,ekv->ecv/dot_general | solution.py:583
  180.0 0.0 copy-done
  180.0 0.0 copy-done.1
  180.1 0.5 convolution_convert_fusion
  180.5 1.3 copy.21
  (1 shorter events, 0.0 us)
Async XLA Ops:
  176.8 3.3 %copy-start = (bf16[8,8,16,512]{3,2,1,0:T(8,128)(2,1)S(1)}, bf16[8,8,16,512]{3,2,1,0:T(8,128)(2,1)}, u32[]{:S(2)}) copy-start(bf16[8,8,16,512]{3,2,1,0:T(8,128)(2,1)} %get-tuple-element.11) | copy-start | bytes 3145732
  176.8 3.3 %copy-start.1 = (bf16[2,4,128,128]{3,2,1,0:T(8,128)(2,1)S(1)}, bf16[2,4,128,128]{3,2,1,0:T(8,128)(2,1)}, u32[]{:S(2)}) copy-start(bf16[2,4,128,128]{3,2,1,0:T(8,128)(2,1)} %get-tuple-element.10) | copy-start | bytes 786436

commit v4 on v3

--- a/solution.py
+++ b/solution.py
@@ -45,47 +45,38 @@
     return copy
 
 
-def scatter_sums(part_ref, got_y, mine, got_z, sems, place, meanwhile=None):
+def wid_sum(part_ref, got_y, mine, got_z, sems, place, meanwhile, finish):
     hi, y, partner, peers = place
-    copies = [
-        send(part_ref.at[:, (y + d) % 4], got_y.at[d - 1], sems.at[0, d - 1], sems.at[1, d - 1], peers[d - 1])
-        for d in (1, 2, 3)
+    near = [
+        [
+            send(part_ref.at[h, (y + d) % 4], got_y.at[d - 1, h], sems.at[0, 3 * h + d - 1],
+                 sems.at[1, 3 * h + d - 1], peers[d - 1])
+            for d in (1, 2, 3)
+        ]
+        for h in range(2)
     ]
-    if meanwhile is not None:
-        meanwhile()
-    for copy in copies:
-        copy.wait()
-
-    def total(h):
+    far = []
+    for h in range(2):
+        for copy in near[h]:
+            copy.wait()
         s = part_ref[h, y].astype(jnp.float32)
         for d in range(3):
             s = s + got_y[d, h].astype(jnp.float32)
-        return s
-
-    mine[...] = total(1 - hi).astype(mine.dtype)
-    copy = send(mine, got_z, sems.at[0, 3], sems.at[1, 3], partner)
-    own = total(hi)
-    copy.wait()
-    return own + got_z[...].astype(jnp.float32)
-
-
-def gather_start(out_ref, sems, base, place):
-    hi, y, partner, peers = place
-    block = out_ref.at[hi, y]
-    far = send(block, block, sems.at[0, base], sems.at[1, base], partner)
-    near = [
+        mine[h] = s.astype(mine.dtype)
+        far.append(send(mine.at[h], got_z.at[h], sems.at[0, 6 + h], sems.at[1, 6 + h], partner))
+    meanwhile()
+    late = []
+    for h in range(2):
+        far[h].wait()
+        late += finish(h, mine[h].astype(jnp.float32) + got_z[h].astype(jnp.float32))
+    for copy in late:
+        copy.wait()
+
+
+def hand_on(block, sems, base, place):
+    peers = place[3]
+    return [
         send(block, block, sems.at[0, base + d], sems.at[1, base + d], peers[d - 1]) for d in (1, 2, 3)
-    ]
-    return far, near
-
-
-def gather_pass(out_ref, sems, base, far, place):
-    hi, y, partner, peers = place
-    far.wait()
-    block = out_ref.at[1 - hi, y]
-    return [
-        send(block, block, sems.at[0, base + 3 + d], sems.at[1, base + 3 + d], peers[d - 1])
-        for d in (1, 2, 3)
     ]
 
 
@@ -96,8 +87,8 @@
 def sum_scratch(slots):
     return [
         pltpu.VMEM((3, 2, slots, BS), jnp.bfloat16),
-        pltpu.VMEM((slots, BS), jnp.bfloat16),
-        pltpu.VMEM((slots, BS), jnp.bfloat16),
+        pltpu.VMEM((2, slots, BS), jnp.bfloat16),
+        pltpu.VMEM((2, slots, BS), jnp.bfloat16),
     ]
 
 
@@ -168,7 +159,7 @@
     return jnp.where(source == col, 1.0, 0.0).astype(jnp.bfloat16)
 
 
-def spread(x_ref, all_ref, pos_ref, stage, got, out_ref, line_sems, plane_sems, place, first, meanwhile=None):
+def spread(x_ref, all_ref, pos_ref, stage, got, out_ref, line_sems, plane_sems, place, first, meanwhile=None, after=None):
     z, q = place
     rows = BS
     features = x_ref.shape[1]
@@ -253,6 +244,8 @@
         return 0
 
     lax.fori_loop(1, LINE, advance, 0)
+    if after is not None:
+        after()
 
     def drain(step, _):
         for c in range(2):
@@ -413,11 +406,18 @@
     return jnp.sum(jnp.where(r == col, row, 0.0), axis=1, keepdims=True)
 
 
-def step_kernel(x_ref, sq_ref, bias_ref, enc_ref, dec_ref,
-                in_ref, resid_ref, codes_ref, dpre_ref, unit_ref, row_ref, small_ref,
+def flat_row(values):
+    r = lax.broadcasted_iota(jnp.int32, (BS, BS), 0)
+    col = lax.broadcasted_iota(jnp.int32, (BS, BS), 1)
+    return jnp.sum(jnp.where(r == col, values, 0.0), axis=0, keepdims=True)
+
+
+def step_kernel(x_ref, bias_ref, enc_ref, dec_ref,
+                in_ref, dpre_ref, grad_ref, small_ref,
                 all_a, stage_a, got_a, line_a, plane_a,
-                sq_y, sq_mine, sq_z,
-                part_b, got_yb, mine_b, got_zb, pre_ref, own_ref, sems_b,
+                sq_ref, sq_y, sq_mine, sq_z,
+                codes_ref, unit_ref, row_ref, resid_ref, raw_ref, scaled_ref,
+                part_b, got_yb, mine_b, got_zb, pre_ref, sems_b,
                 terms_ref, res_ref, stage_c, got_c, sums, from_left, from_right, right_sum, left_sum,
                 line_c, plane_c,
                 all_d, stage_d, got_d, line_d, plane_d,
@@ -430,22 +430,32 @@
     f32, bf16 = jnp.float32, jnp.bfloat16
     greet(place, wid)
 
-    sq_copies = [
-        send(sq_ref, sq_y.at[d - 1], sems_b.at[0, 10 + d], sems_b.at[1, 10 + d], peers[d - 1])
-        for d in (1, 2, 3)
-    ]
+    def sq_copy(d):
+        return pltpu.make_async_remote_copy(
+            src_ref=sq_ref, dst_ref=sq_y.at[d - 1], send_sem=sems_b.at[0, 13 + d],
+            recv_sem=sems_b.at[1, 13 + d], device_id={"wid": peers[d - 1]}, device_id_type=MESH,
+        )
+
     sq_far = pltpu.make_async_remote_copy(
-        src_ref=sq_mine, dst_ref=sq_z, send_sem=sems_b.at[0, 14], recv_sem=sems_b.at[1, 14],
+        src_ref=sq_mine, dst_ref=sq_z, send_sem=sems_b.at[0, 17], recv_sem=sems_b.at[1, 17],
         device_id={"wid": partner}, device_id_type=MESH,
     )
 
+    def square():
+        for k in range(8):
+            wide = dec_ref[k].astype(f32)
+            total = jnp.sum(wide * wide, axis=1, keepdims=True)
+            sq_ref[k : k + 1, :] = flat_row(total)
+        for d in (1, 2, 3):
+            sq_copy(d).start()
+
     def sum_squares():
-        for copy in sq_copies:
-            copy.wait()
+        for d in (1, 2, 3):
+            sq_copy(d).wait()
         sq_mine[...] = sq_ref[...] + sq_y[0] + sq_y[1] + sq_y[2]
         sq_far.start()
 
-    spread(x_ref, all_a, pos_ref, stage_a, got_a, in_ref, line_a, plane_a, place, True, sum_squares)
+    spread(x_ref, all_a, pos_ref, stage_a, got_a, in_ref, line_a, plane_a, place, True, square, sum_squares)
 
     for k in range(8):
         part_b[k // 4, k % 4] = jnp.dot(
@@ -457,19 +467,20 @@
         row_ref[...] = jnp.sqrt(sq_mine[...] + sq_z[...] + EPS)
         for k in range(8):
             norm = column(row_ref[k : k + 1, :])
-            unit_ref[k] = (dec_ref[k].astype(f32) / norm).astype(bf16)
-
-    mine = hi * 4 + y
-    preact = scatter_sums(part_b, got_yb, mine_b, got_zb, sems_b, wid, normalize) + bias_ref[mine]
-    pre_ref[...] = preact
-    live = in_ref[mine].reshape(BS, features)[:, 0:1].astype(f32) < 1.5
-    codes = jnp.where(live, gelu(preact), 0.0).astype(bf16)
-    own_ref[...] = codes
-    codes_ref[hi, y] = codes
-    far, near = gather_start(codes_ref, sems_b, 4, wid)
-    late = gather_pass(codes_ref, sems_b, 4, far, wid)
-    for copy in near + late:
-        copy.wait()
+            unit = (dec_ref[k].astype(f32) / norm).astype(bf16)
+            unit_ref[k] = unit
+            scaled_ref[k] = unit.astype(f32) / norm
+
+    def live(h):
+        return in_ref[h * 4 + y].reshape(BS, features)[:, 0:1].astype(f32) < 1.5
+
+    def encode(h, total):
+        preact = total + bias_ref[h * 4 + y]
+        pre_ref[h] = preact
+        codes_ref[h, y] = jnp.where(live(h), gelu(preact), 0.0).astype(bf16)
+        return hand_on(codes_ref.at[h, y], sems_b, 7 + 3 * h, wid)
+
+    wid_sum(part_b, got_yb, mine_b, got_zb, sems_b, wid, normalize, encode)
 
     for k in range(8):
         terms_ref[k] = (
@@ -486,20 +497,31 @@
             resid_ref[k].reshape(BS, features), unit_ref[k], (((1,), (1,)), ((), ())),
             preferred_element_type=f32,
         ).astype(bf16)
-    dcode = scatter_sums(part_e, got_ye, mine_e, got_ze, sems_e, wid)
-    dpre = jnp.where(live, dcode * gelu_slope(pre_ref[...]), 0.0)
-    dpre_ref[hi, y] = dpre.astype(bf16)
-    far, near = gather_start(dpre_ref, sems_e, 4, wid)
-    along = jnp.sum(own_ref[...].astype(f32) * dcode, axis=0, keepdims=True)
-    bias_grad = jnp.sum(dpre, axis=0, keepdims=True)
-    row = lax.broadcasted_iota(jnp.int32, (8, BS), 0)
-    small_ref[hi, y] = jnp.where(row == 0, along, bias_grad)
-    small_far, small_near = gather_start(small_ref, sems_e, 11, wid)
-    lax.fori_loop(0, LINE, drain, 0)
-    late = gather_pass(dpre_ref, sems_e, 4, far, wid)
-    small_late = gather_pass(small_ref, sems_e, 11, small_far, wid)
-    for copy in near + late + small_near + small_late:
-        copy.wait()
+
+    def decoder_sums():
+        for k in range(8):
+            raw = lax.dot_general(
+                codes_ref[k // 4, k % 4], resid_ref[k].reshape(BS, features), (((0,), (0,)), ((), ())),
+                preferred_element_type=f32,
+            )
+            raw_ref[k] = raw / column(row_ref[k : k + 1, :])
+        lax.fori_loop(0, LINE, drain, 0)
+
+    def differentiate(h, dcode):
+        dpre = jnp.where(live(h), dcode * gelu_slope(pre_ref[h]), 0.0)
+        dpre_ref[h, y] = dpre.astype(bf16)
+        along = jnp.sum(codes_ref[h, y].astype(f32) * dcode, axis=0, keepdims=True)
+        bias_grad = jnp.sum(dpre, axis=0, keepdims=True)
+        row = lax.broadcasted_iota(jnp.int32, (8, BS), 0)
+        small_ref[h, y] = jnp.where(row == 0, along, bias_grad)
+        return hand_on(dpre_ref.at[h, y], sems_e, 7 + 3 * h, wid) + hand_on(
+            small_ref.at[h, y], sems_e, 13 + 3 * h, wid
+        )
+
+    wid_sum(part_e, got_ye, mine_e, got_ze, sems_e, wid, decoder_sums, differentiate)
+    for k in range(8):
+        along = column(small_ref[k // 4, k % 4, 0:1, :])
+        grad_ref[k] = (raw_ref[k] - along * scaled_ref[k]).astype(bf16)
 
 
 def slots_buffer(features):
@@ -510,7 +532,7 @@
     return [pltpu.SemaphoreType.DMA((2, 2, LINE, 2)), pltpu.SemaphoreType.DMA((2, LINE, PLANE - 1))]
 
 
-def run_step(x, sq, bias, encoder, decoder):
+def run_step(x, bias, encoder, decoder):
     rows, features = BS, x.shape[1]
     f32, bf16 = jnp.float32, jnp.bfloat16
     slots = 2 * LINE * PLANE
@@ -519,25 +541,24 @@
     wid_part = pltpu.VMEM((2, 4, slots, BS), bf16)
     sq_block = pltpu.VMEM((8, BS), f32)
     row_total = pltpu.VMEM((rows, features), f32)
+    latents = pltpu.VMEM((8, BS, features), f32)
     return pl.pallas_call(
         step_kernel,
         out_shape=(
             jax.ShapeDtypeStruct((8, PLANE, 16, features), bf16),
-            jax.ShapeDtypeStruct((8, PLANE, 16, features), bf16),
-            jax.ShapeDtypeStruct((2, 4, slots, BS), bf16),
             jax.ShapeDtypeStruct((2, 4, slots, BS), bf16),
             jax.ShapeDtypeStruct((8, BS, features), bf16),
-            jax.ShapeDtypeStruct((8, BS), f32),
             jax.ShapeDtypeStruct((2, 4, 8, BS), f32),
         ),
-        in_specs=vmem(5),
-        out_specs=tuple(vmem(7)),
+        in_specs=vmem(4),
+        out_specs=tuple(vmem(4)),
         scratch_shapes=[pltpu.VMEM((LINE, x.shape[0], features), bf16), slot, slot]
         + lat_sems()
-        + [pltpu.VMEM((3, 8, BS), f32), sq_block, sq_block]
+        + [sq_block, pltpu.VMEM((3, 8, BS), f32), sq_block, sq_block]
+        + [wid_part, pltpu.VMEM((8, BS, features), bf16), sq_block, slot, latents, latents]
         + [wid_part]
         + sum_scratch(slots)
-        + [pltpu.VMEM((slots, BS), f32), pltpu.VMEM((slots, BS), bf16), pltpu.SemaphoreType.DMA((2, 15))]
+        + [pltpu.VMEM((2, slots, BS), f32), pltpu.SemaphoreType.DMA((2, 18))]
         + [slot, pltpu.VMEM((rows, features), bf16), slot, slot]
         + [row_blocks, row_blocks, row_blocks, row_total, row_total]
         + lat_sems()
@@ -545,10 +566,10 @@
         + lat_sems()
         + [wid_part]
         + sum_scratch(slots)
-        + [pltpu.SemaphoreType.DMA((2, 18)), pltpu.VMEM((LINE, 8, BS), f32)],
+        + [pltpu.SemaphoreType.DMA((2, 20)), pltpu.VMEM((LINE, 8, BS), f32)],
         compiler_params=pltpu.CompilerParams(collective_id=0, has_side_effects=True),
         name="step",
-    )(x, sq, bias, encoder, decoder)
+    )(x, bias, encoder, decoder)
 
 
 def body(activations, block_ids, alive_tallies, encoder, encoder_bias, decoder):
@@ -566,30 +587,20 @@
     high = jnp.where(alive, position >> 3, 255)
     codes_of_rows = jnp.concatenate([high, position & 7], axis=1).T.astype(jnp.bfloat16)
     extra = jnp.pad(codes_of_rows, ((0, 8), (0, features - rows)))
-    local_sq = jnp.sum(jnp.square(decoder.astype(f32)), axis=1).reshape(8, BS)
-    incoming, resid_in, codes, dpre, unit, row_norm, small = run_step(
+    incoming, dpre, decoder_grad, small = run_step(
         jnp.concatenate([activations, extra], axis=0),
-        local_sq,
         encoder_bias.reshape(8, 1, BS),
         encoder,
         decoder.reshape(8, BS, features),
     )
     incoming = incoming.reshape(8, lat * 2, features)
-    resid_in = resid_in.reshape(8, lat * 2, features)
-    codes = codes.reshape(8, lat * 2, BS)
     dpre = dpre.reshape(8, lat * 2, BS)
-    small = small.reshape(8, 8, BS)
-    row_norm = row_norm[:, :, None]
-    raw = jnp.einsum("ekc,ekv->ecv", codes, resid_in, preferred_element_type=f32)
-    along = small[:, 0, :, None]
-    bias_grad = small[:, 1].reshape(8 * BS)
+    decoder_grad = decoder_grad.reshape(8 * BS, features)
+    bias_grad = small.reshape(8, 8, BS)[:, 1].reshape(8 * BS)
     encoder_grad = (
         jnp.einsum("kiy,kif->ykf", incoming, dpre, preferred_element_type=f32)
         .reshape(features, 8 * BS)
         .astype(jnp.bfloat16)
-    )
-    decoder_grad = (
-        ((raw - along * unit.astype(f32)) / row_norm).astype(jnp.bfloat16).reshape(8 * BS, features)
     )
     return encoder_grad, decoder_grad, bias_grad
 

time: 183 us -> 165 us (0.902)
  Pallas kernels: 169 us -> 155 us
  other arithmetic: 4.66 us -> 2.57 us
  matrix products: 3.76 us -> 1.8 us
    pallas_call x1, Pallas kernels: 169 us -> 155 us  [run_step(): pl.pallas_call(step_kernel, out_shape=(jax.ShapeDtypeStruct((8, PLANE, 16...]
    dot_general x1 -> x0, matrix products: 3.27 us -> none  [body(): jnp.einsum('ekc,ekv->ecv', codes, resid_in, preferred_element_type=f32)]
    reduce_sum x1 -> x0, other arithmetic: 2.09 us -> none  [body(): local_sq = jnp.sum(jnp.square(decoder.astype(f32)), axis=1).reshape(8, BS)]
where the time goes in v4:
time: 165 us
  Pallas kernels  155 us (94%)
  local copies, waits for them, and re-layouts  4.71 us (3%)
  other arithmetic  2.57 us (2%)
  matrix products  1.8 us (1%)
    pallas_call x1, Pallas kernels, run_step(): pl.pallas_call(step_kernel, out_shape=(jax.ShapeDtypeStruct((8, PLANE, 16...  155 us

profile of v4, /device:TPU:1, one launch (start us, length us, event | category | flops | bytes accessed | tf_op | source)
XLA Modules:
  0.0 164.8 jit_solution(10438502470701543137)
XLA Ops:
  0.6 0.8 copy.15
  1.4 0.1 eq.15
  1.5 0.3 convert_reduce_fusion
  1.8 0.1 reshape.32
  1.9 0.1 copy.16
  2.0 0.7 select_convert_fusion
  2.7 1.6 fusion.2.x_ref
  4.3 155.0 %step.1 = (bf16[8,8,16,512]{3,2,1,0:T(8,128)(2,1)}, bf16[2,4,128,128]{3,2,1,0:T(8,128)(2,1)}, bf16[8,128,512]{2,1,0:T(8,128)(2,1)}, f32[2,4,8,128]{3,2,1,0:T(8,128)}) custom-call(bf16[144,512]{1,0:T(8,128)(2,1)} %fusion.2.x_ref, f32[8,1,128]{2,1,0:T(1,128)} %bitcast.19, bf16[512,1024]{1,0:T(8,128)(2,1)} %enc_ref.1, bf16[8,128,512]{2,1,0:T(8,128)(2,1)} %bitcast.15), custom_call_target="tpu_custom_call" | custom-call | tf_op jit(solution)/shard_map/step/pallas_call | solution.py:545
  159.3 1.8 %convolution_convert_fusion = bf16[8,128,512]{2,1,0:T(8,128)(2,1)S(1)} fusion(bf16[8,128,128]{2,1,0:T(8,128)(2,1)} %bitcast.18, bf16[8,128,512]{2,1,0:T(8,128)(2,1)} %bitcast.17), kind=kOutput, calls=%fused_computation | convolution fusion | flops 134742016 | bytes 2359296 | tf_op jit(solution)/shard_map/kiy,kif->ykf/dot_general | solution.py:601
  161.1 0.0 copy-start
  161.1 1.3 copy.18
  162.4 1.4 slice.4
  163.8 0.0 copy-done
  163.8 1.0 copy.21
  (1 shorter events, 0.0 us)
Async XLA Ops:
  161.1 2.7 %copy-start = (bf16[8,128,512]{2,1,0:T(8,128)(2,1)S(1)}, bf16[8,128,512]{2,1,0:T(8,128)(2,1)}, u32[]{:S(2)}) copy-start(bf16[8,128,512]{2,1,0:T(8,128)(2,1)} %get-tuple-element.9) | copy-start | bytes 3145732

commit v5 on v4

--- a/solution.py
+++ b/solution.py
@@ -12,6 +12,7 @@
 FILLER = 2.0
 LINE = 8
 PLANE = 8
+PIECES = 4
 MESH = pl.DeviceIdType.MESH
 
 
@@ -140,8 +141,8 @@
     )
 
 
-def half(c, features):
-    return pl.ds(c * (features // 2), features // 2)
+def piece(c):
+    return pl.ds(c * (BS // PIECES), BS // PIECES)
 
 
 def slot_matrix(local):
@@ -159,17 +160,23 @@
     return jnp.where(source == col, 1.0, 0.0).astype(jnp.bfloat16)
 
 
-def spread(x_ref, all_ref, pos_ref, stage, got, out_ref, line_sems, plane_sems, place, first, meanwhile=None, after=None):
+def spread(x_ref, all_ref, pos_ref, stage, got, out_ref, line_sems, plane_sems, place, own_code=None,
+           code_ref=None, meanwhile=None, after=None):
     z, q = place
-    rows = BS
     features = x_ref.shape[1]
-
-    def line_copy(b, step, c, way, src=None):
-        src = all_ref.at[b] if src is None else src
-        height = pl.ds(0, rows if c else x_ref.shape[0])
+    first = own_code is not None
+    pieces = PIECES + first
+
+    def line_copy(b, step, c, way, own=False):
+        if first and c == 0:
+            src, dst = own_code if own else code_ref.at[b], code_ref.at[b]
+        else:
+            part = piece(c - first)
+            src = x_ref.at[part] if own else all_ref.at[b, part]
+            dst = all_ref.at[b, part]
         return lat_copy(
-            src.at[height, half(c, features)],
-            all_ref.at[b, height, half(c, features)],
+            src,
+            dst,
             line_sems.at[0, way, step, c],
             line_sems.at[1, way, step, c],
             z + 1 - 2 * way,
@@ -182,16 +189,16 @@
             stage.at[b, to], got.at[q, b], plane_sems.at[0, b, e - 1], plane_sems.at[1, b, e - 1], z, to
         )
 
-    def select(b, ref):
+    def select(b, ref, codes):
         if first:
-            code = ref[rows : rows + 8, 0:BS].astype(jnp.float32)
+            code = codes[0:8, :].astype(jnp.float32)
             base = (z * BS).astype(jnp.float32)
             local = code[0:4] * 8.0 + code[4:8] - base
             pos_ref[b] = jnp.concatenate([local, local], axis=0)
         else:
             local = pos_ref[b]
         hit = slot_matrix(local)
-        picked = jnp.dot(hit.astype(jnp.bfloat16), ref[0:rows, :], preferred_element_type=jnp.float32)
+        picked = jnp.dot(hit.astype(jnp.bfloat16), ref[...], preferred_element_type=jnp.float32)
         if first:
             filled = jnp.sum(hit, axis=1, keepdims=True)
             picked = jnp.where(filled > 0.5, picked, FILLER)
@@ -201,22 +208,22 @@
             plane_copy(b, e).start()
 
     can_right, can_left = z < LINE - 1, z > 0
-    for c in range(2):
+    for c in range(pieces):
         @pl.when(can_right)
         def _():
-            line_copy(z, 0, c, 0, x_ref).start()
+            line_copy(z, 0, c, 0, True).start()
 
         @pl.when(can_left)
         def _():
-            line_copy(z, 0, c, 1, x_ref).start()
-
-    select(z, x_ref)
+            line_copy(z, 0, c, 1, True).start()
+
+    select(z, x_ref, own_code)
     if meanwhile is not None:
         meanwhile()
 
     def advance(step, _):
         from_left, from_right = z - step, z + step
-        for c in range(2):
+        for c in range(pieces):
             @pl.when(from_left >= 0)
             def _():
                 line_copy(from_left, step - 1, c, 0).wait_recv()
@@ -235,11 +242,11 @@
 
         @pl.when(from_left >= 0)
         def _():
-            select(from_left, all_ref.at[from_left])
+            select(from_left, all_ref.at[from_left], code_ref.at[from_left] if first else None)
 
         @pl.when(from_right < LINE)
         def _():
-            select(from_right, all_ref.at[from_right])
+            select(from_right, all_ref.at[from_right], code_ref.at[from_right] if first else None)
 
         return 0
 
@@ -248,7 +255,7 @@
         after()
 
     def drain(step, _):
-        for c in range(2):
+        for c in range(pieces):
             @pl.when(jnp.logical_and(z - step >= 0, can_right))
             def _():
                 line_copy(z - step, step, c, 0).wait_send()
@@ -294,8 +301,8 @@
     def line_copy(d, far, c, way):
         land = from_right if way else from_left
         return lat_copy(
-            sums.at[d, :, half(c, features)],
-            land.at[d, :, half(c, features)],
+            sums.at[d, piece(c)],
+            land.at[d, piece(c)],
             line_sems.at[0, way, far, c],
             line_sems.at[1, way, far, c],
             z + 1 - 2 * way,
@@ -341,17 +348,17 @@
         def _():
             left_sum[...] = partial(left)
 
-        for c in range(2):
-            part = half(c, features)
+        for c in range(PIECES):
+            part = piece(c)
 
             @pl.when(go_right)
             def _():
                 @pl.when(z > 0)
                 def _():
                     line_copy(right, far + 1, c, 0).wait_recv()
-                    right_sum[:, part] += from_left[right, :, part].astype(jnp.float32)
-
-                sums[right, :, part] = right_sum[:, part].astype(jnp.bfloat16)
+                    right_sum[part, :] += from_left[right, part, :].astype(jnp.float32)
+
+                sums[right, part, :] = right_sum[part, :].astype(jnp.bfloat16)
                 line_copy(right, far, c, 0).start()
 
             @pl.when(go_left)
@@ -359,9 +366,9 @@
                 @pl.when(z < LINE - 1)
                 def _():
                     line_copy(left, far + 1, c, 1).wait_recv()
-                    left_sum[:, part] += from_right[left, :, part].astype(jnp.float32)
-
-                sums[left, :, part] = left_sum[:, part].astype(jnp.bfloat16)
+                    left_sum[part, :] += from_right[left, part, :].astype(jnp.float32)
+
+                sums[left, part, :] = left_sum[part, :].astype(jnp.bfloat16)
                 line_copy(left, far, c, 1).start()
 
         return 0
@@ -371,20 +378,20 @@
 
     @pl.when(z > 0)
     def _():
-        for c in range(2):
+        for c in range(PIECES):
             line_copy(z, 1, c, 0).wait_recv()
         right_sum[...] += from_left[z].astype(jnp.float32)
 
     @pl.when(z < LINE - 1)
     def _():
-        for c in range(2):
+        for c in range(PIECES):
             line_copy(z, 1, c, 1).wait_recv()
         right_sum[...] += from_right[z].astype(jnp.float32)
 
     res_ref[...] = right_sum[...].astype(jnp.bfloat16)
 
     def drain(far, _):
-        for c in range(2):
+        for c in range(PIECES):
             @pl.when(jnp.logical_and(z + far < LINE, far > 0))
             def _():
                 line_copy(z + far, far, c, 0).wait_send()
@@ -412,9 +419,9 @@
     return jnp.sum(jnp.where(r == col, values, 0.0), axis=0, keepdims=True)
 
 
-def step_kernel(x_ref, bias_ref, enc_ref, dec_ref,
-                in_ref, dpre_ref, grad_ref, small_ref,
-                all_a, stage_a, got_a, line_a, plane_a,
+def step_kernel(x_ref, code_ref, bias_ref, enc_ref, dec_ref,
+                enc_grad_ref, grad_ref, bias_grad_ref,
+                in_ref, turned_ref, dpre_ref, small_ref, all_a, code_all, stage_a, got_a, line_a, plane_a,
                 sq_ref, sq_y, sq_mine, sq_z,
                 codes_ref, unit_ref, row_ref, resid_ref, raw_ref, scaled_ref,
                 part_b, got_yb, mine_b, got_zb, pre_ref, sems_b,
@@ -425,7 +432,6 @@
     place = lat_place()
     wid = wid_place()
     hi, y, partner, peers = wid
-    rows = BS
     features = x_ref.shape[1]
     f32, bf16 = jnp.float32, jnp.bfloat16
     greet(place, wid)
@@ -455,7 +461,8 @@
         sq_mine[...] = sq_ref[...] + sq_y[0] + sq_y[1] + sq_y[2]
         sq_far.start()
 
-    spread(x_ref, all_a, pos_ref, stage_a, got_a, in_ref, line_a, plane_a, place, True, square, sum_squares)
+    spread(x_ref, all_a, pos_ref, stage_a, got_a, in_ref, line_a, plane_a, place, code_ref, code_all,
+           square, sum_squares)
 
     for k in range(8):
         part_b[k // 4, k % 4] = jnp.dot(
@@ -488,9 +495,9 @@
             .astype(bf16)
             .reshape(PLANE, 16, features)
         )
-    drain = collect(terms_ref, x_ref.at[0:rows, :], pos_ref, res_ref, stage_c, got_c, sums, from_left,
+    drain = collect(terms_ref, x_ref, pos_ref, res_ref, stage_c, got_c, sums, from_left,
                     from_right, right_sum, left_sum, line_c, plane_c, place)
-    spread(res_ref, all_d, pos_ref, stage_d, got_d, resid_ref, line_d, plane_d, place, False)
+    spread(res_ref, all_d, pos_ref, stage_d, got_d, resid_ref, line_d, plane_d, place)
 
     for k in range(8):
         part_e[k // 4, k % 4] = lax.dot_general(
@@ -505,6 +512,7 @@
                 preferred_element_type=f32,
             )
             raw_ref[k] = raw / column(row_ref[k : k + 1, :])
+            turned_ref[k] = in_ref[k].reshape(BS, features).T
         lax.fori_loop(0, LINE, drain, 0)
 
     def differentiate(h, dcode):
@@ -520,6 +528,10 @@
 
     wid_sum(part_e, got_ye, mine_e, got_ze, sems_e, wid, decoder_sums, differentiate)
     for k in range(8):
+        enc_grad_ref[:, k * BS : (k + 1) * BS] = jnp.dot(
+            turned_ref[k], dpre_ref[k // 4, k % 4], preferred_element_type=f32
+        ).astype(bf16)
+        bias_grad_ref[k : k + 1, :] = small_ref[k // 4, k % 4, 1:2, :]
         along = column(small_ref[k // 4, k % 4, 0:1, :])
         grad_ref[k] = (raw_ref[k] - along * scaled_ref[k]).astype(bf16)
 
@@ -529,10 +541,10 @@
 
 
 def lat_sems():
-    return [pltpu.SemaphoreType.DMA((2, 2, LINE, 2)), pltpu.SemaphoreType.DMA((2, LINE, PLANE - 1))]
-
-
-def run_step(x, bias, encoder, decoder):
+    return [pltpu.SemaphoreType.DMA((2, 2, LINE, PIECES + 1)), pltpu.SemaphoreType.DMA((2, LINE, PLANE - 1))]
+
+
+def run_step(x, codes, bias, encoder, decoder):
     rows, features = BS, x.shape[1]
     f32, bf16 = jnp.float32, jnp.bfloat16
     slots = 2 * LINE * PLANE
@@ -545,14 +557,15 @@
     return pl.pallas_call(
         step_kernel,
         out_shape=(
-            jax.ShapeDtypeStruct((8, PLANE, 16, features), bf16),
-            jax.ShapeDtypeStruct((2, 4, slots, BS), bf16),
+            jax.ShapeDtypeStruct((features, 8 * BS), bf16),
             jax.ShapeDtypeStruct((8, BS, features), bf16),
-            jax.ShapeDtypeStruct((2, 4, 8, BS), f32),
+            jax.ShapeDtypeStruct((8, BS), f32),
         ),
-        in_specs=vmem(4),
-        out_specs=tuple(vmem(4)),
-        scratch_shapes=[pltpu.VMEM((LINE, x.shape[0], features), bf16), slot, slot]
+        in_specs=vmem(5),
+        out_specs=tuple(vmem(3)),
+        scratch_shapes=[slot, pltpu.VMEM((8, features, BS), bf16), wid_part]
+        + [pltpu.VMEM((2, 4, 8, BS), f32)]
+        + [row_blocks, pltpu.VMEM((LINE, 16, BS), bf16), slot, slot]
         + lat_sems()
         + [sq_block, pltpu.VMEM((3, 8, BS), f32), sq_block, sq_block]
         + [wid_part, pltpu.VMEM((8, BS, features), bf16), sq_block, slot, latents, latents]
@@ -569,7 +582,7 @@
         + [pltpu.SemaphoreType.DMA((2, 20)), pltpu.VMEM((LINE, 8, BS), f32)],
         compiler_params=pltpu.CompilerParams(collective_id=0, has_side_effects=True),
         name="step",
-    )(x, bias, encoder, decoder)
+    )(x, codes, bias, encoder, decoder)
 
 
 def body(activations, block_ids, alive_tallies, encoder, encoder_bias, decoder):
@@ -586,22 +599,12 @@
     position = block_ids * 2 + rank
     high = jnp.where(alive, position >> 3, 255)
     codes_of_rows = jnp.concatenate([high, position & 7], axis=1).T.astype(jnp.bfloat16)
-    extra = jnp.pad(codes_of_rows, ((0, 8), (0, features - rows)))
-    incoming, dpre, decoder_grad, small = run_step(
-        jnp.concatenate([activations, extra], axis=0),
-        encoder_bias.reshape(8, 1, BS),
-        encoder,
-        decoder.reshape(8, BS, features),
+    extra = jnp.pad(codes_of_rows, ((0, 8), (0, 0)))
+    encoder_grad, decoder_grad, bias_grad = run_step(
+        activations, extra, encoder_bias.reshape(8, 1, BS), encoder, decoder.reshape(8, BS, features)
     )
-    incoming = incoming.reshape(8, lat * 2, features)
-    dpre = dpre.reshape(8, lat * 2, BS)
     decoder_grad = decoder_grad.reshape(8 * BS, features)
-    bias_grad = small.reshape(8, 8, BS)[:, 1].reshape(8 * BS)
-    encoder_grad = (
-        jnp.einsum("kiy,kif->ykf", incoming, dpre, preferred_element_type=f32)
-        .reshape(features, 8 * BS)
-        .astype(jnp.bfloat16)
-    )
+    bias_grad = bias_grad.reshape(8 * BS)
     return encoder_grad, decoder_grad, bias_grad
 
 

time: 165 us -> 160 us (0.970)
  Pallas kernels: 155 us -> 152 us
  other arithmetic: 2.57 us -> 0.28 us
  matrix products: 1.8 us -> 0 us
    pallas_call x1, Pallas kernels: 155 us -> 152 us  [run_step(): pl.pallas_call(step_kernel, out_shape=(jax.ShapeDtypeStruct((features, 8...]
    unnamed x5 -> x12, local copies, waits for them, and re-layouts: 3.08 us -> 5.3 us
    dot_general x1 -> x0, matrix products: 1.8 us -> none  [body(): jnp.einsum('kiy,kif->ykf', incoming, dpre, preferred_element_type=f32)]
where the time goes in v5:
time: 160 us; the launch traced here: 159 us
  Pallas kernels  152 us (95%)
  local copies, waits for them, and re-layouts  6.17 us (4%)
    pallas_call x1, Pallas kernels, run_step(): pl.pallas_call(step_kernel, out_shape=(jax.ShapeDtypeStruct((features, 8...  152 us
    unnamed x12, local copies, waits for them, and re-layouts  5.3 us

profile of v5, /device:TPU:1, one launch (start us, length us, event | category | flops | bytes accessed | tf_op | source)
XLA Modules:
  0.0 159.5 jit_solution(9591235198692636509)
XLA Ops:
  0.6 0.0 copy-start.1
  0.6 0.7 copy-done.1
  1.3 0.1 copy.11
  1.4 0.1 eq.15
  1.5 0.3 convert_reduce_fusion
  1.8 0.1 reshape.24
  1.9 0.0 copy-start.3
  1.9 0.1 copy.12
  2.0 0.6 copy-done.3
  2.6 0.6 pad.4.code_ref
  3.2 152.3 %step.1 = (bf16[512,1024]{1,0:T(8,128)(2,1)}, bf16[8,128,512]{2,1,0:T(8,128)(2,1)}, f32[8,128]{1,0:T(8,128)}) custom-call(bf16[128,512]{1,0:T(8,128)(2,1)} %x_ref.1, bf16[16,128]{1,0:T(8,128)(2,1)} %pad.4.code_ref, f32[8,1,128]{2,1,0:T(1,128)} %bitcast.8, bf16[512,1024]{1,0:T(8,128)(2,1)} %enc_ref.1, bf16[8,128,512]{2,1,0:T(8,128)(2,1)} %bitcast.6), custom_call_target="tpu_custom_call" | custom-call | tf_op jit(solution)/shard_map/step/pallas_call | solution.py:557
  155.5 0.0 copy-start
  155.6 2.4 %copy.16 = bf16[512,1024]{1,0:T(8,128)(2,1)} copy(bf16[512,1024]{1,0:T(8,128)(2,1)} %get-tuple-element.14) | data formatting | bytes 2097152
  157.9 0.0 copy-done
  157.9 0.0 copy-start.2
  157.9 1.0 copy.17
  158.9 0.0 copy-done.2
  158.9 0.6 copy.18
  (2 shorter events, 0.0 us)
Async XLA Ops:
  0.6 0.7 copy-start.1
  1.9 0.7 copy-start.3
  155.5 2.4 %copy-start = (bf16[8,128,512]{2,1,0:T(8,128)(2,1)S(1)}, bf16[8,128,512]{2,1,0:T(8,128)(2,1)}, u32[]{:S(2)}) copy-start(bf16[8,128,512]{2,1,0:T(8,128)(2,1)} %get-tuple-element.7) | copy-start | bytes 3145732
  157.9 1.0 copy-start.2

commit v6 on v5

--- a/solution.py
+++ b/solution.py
@@ -46,16 +46,16 @@
     return copy
 
 
-def wid_sum(part_ref, got_y, mine, got_z, sems, place, meanwhile, finish):
+def wid_sum(part_ref, got_y, mine, got_z, sems, place, fill, meanwhile, finish):
     hi, y, partner, peers = place
-    near = [
-        [
+    near = []
+    for h in range(2):
+        fill(h)
+        near.append([
             send(part_ref.at[h, (y + d) % 4], got_y.at[d - 1, h], sems.at[0, 3 * h + d - 1],
                  sems.at[1, 3 * h + d - 1], peers[d - 1])
             for d in (1, 2, 3)
-        ]
-        for h in range(2)
-    ]
+        ])
     far = []
     for h in range(2):
         for copy in near[h]:
@@ -254,27 +254,32 @@
     if after is not None:
         after()
 
-    def drain(step, _):
-        for c in range(pieces):
-            @pl.when(jnp.logical_and(z - step >= 0, can_right))
-            def _():
-                line_copy(z - step, step, c, 0).wait_send()
-
-            @pl.when(jnp.logical_and(z + step < LINE, can_left))
-            def _():
-                line_copy(z + step, step, c, 1).wait_send()
-
-        for e in range(1, PLANE):
-            plane_copy(step, e).wait()
-        return 0
-
-    lax.fori_loop(0, LINE, drain, 0)
     swap = swap_matrix()
-    for source in range(PLANE):
+    for e in range(PLANE):
+        source = (q + PLANE - e) % PLANE
+        if e > 0:
+            for b in range(LINE):
+                plane_copy(b, e).wait_recv()
         block = jnp.dot(
             swap, got[source].reshape(BS, features), preferred_element_type=jnp.float32
         ).astype(jnp.bfloat16)
         out_ref[:, source] = block.reshape(8, 16, features)
+
+    def drain(step, _):
+        for c in range(pieces):
+            @pl.when(jnp.logical_and(z - step >= 0, can_right))
+            def _():
+                line_copy(z - step, step, c, 0).wait_send()
+
+            @pl.when(jnp.logical_and(z + step < LINE, can_left))
+            def _():
+                line_copy(z + step, step, c, 1).wait_send()
+
+        for e in range(1, PLANE):
+            plane_copy(step, e).wait_send()
+        return 0
+
+    lax.fori_loop(0, LINE, drain, 0)
 
 
 def collect(terms_ref, act_ref, pos_ref, res_ref, stage, got, sums, from_left, from_right, right_sum,
@@ -464,10 +469,12 @@
     spread(x_ref, all_a, pos_ref, stage_a, got_a, in_ref, line_a, plane_a, place, code_ref, code_all,
            square, sum_squares)
 
-    for k in range(8):
-        part_b[k // 4, k % 4] = jnp.dot(
-            in_ref[k].reshape(BS, features), enc_ref[:, k * BS : (k + 1) * BS], preferred_element_type=f32
-        ).astype(bf16)
+    def partial_preact(h):
+        for k in range(4 * h, 4 * h + 4):
+            part_b[h, k % 4] = jnp.dot(
+                in_ref[k].reshape(BS, features), enc_ref[:, k * BS : (k + 1) * BS],
+                preferred_element_type=f32,
+            ).astype(bf16)
 
     def normalize():
         sq_far.wait()
@@ -487,7 +494,7 @@
         codes_ref[h, y] = jnp.where(live(h), gelu(preact), 0.0).astype(bf16)
         return hand_on(codes_ref.at[h, y], sems_b, 7 + 3 * h, wid)
 
-    wid_sum(part_b, got_yb, mine_b, got_zb, sems_b, wid, normalize, encode)
+    wid_sum(part_b, got_yb, mine_b, got_zb, sems_b, wid, partial_preact, normalize, encode)
 
     for k in range(8):
         terms_ref[k] = (
@@ -499,11 +506,12 @@
                     from_right, right_sum, left_sum, line_c, plane_c, place)
     spread(res_ref, all_d, pos_ref, stage_d, got_d, resid_ref, line_d, plane_d, place)
 
-    for k in range(8):
-        part_e[k // 4, k % 4] = lax.dot_general(
-            resid_ref[k].reshape(BS, features), unit_ref[k], (((1,), (1,)), ((), ())),
-            preferred_element_type=f32,
-        ).astype(bf16)
+    def partial_dcode(h):
+        for k in range(4 * h, 4 * h + 4):
+            part_e[h, k % 4] = lax.dot_general(
+                resid_ref[k].reshape(BS, features), unit_ref[k], (((1,), (1,)), ((), ())),
+                preferred_element_type=f32,
+            ).astype(bf16)
 
     def decoder_sums():
         for k in range(8):
@@ -526,7 +534,7 @@
             small_ref.at[h, y], sems_e, 13 + 3 * h, wid
         )
 
-    wid_sum(part_e, got_ye, mine_e, got_ze, sems_e, wid, decoder_sums, differentiate)
+    wid_sum(part_e, got_ye, mine_e, got_ze, sems_e, wid, partial_dcode, decoder_sums, differentiate)
     for k in range(8):
         enc_grad_ref[:, k * BS : (k + 1) * BS] = jnp.dot(
             turned_ref[k], dpre_ref[k // 4, k % 4], preferred_element_type=f32

time: 160 us -> 159 us (level)
  no operation moved by 1% of the time
where the time goes in v6:
time: 159 us
  Pallas kernels  151 us (95%)
  local copies, waits for them, and re-layouts  6.17 us (4%)
    pallas_call x1, Pallas kernels, run_step(): pl.pallas_call(step_kernel, out_shape=(jax.ShapeDtypeStruct((features, 8...  151 us
    unnamed x12, local copies, waits for them, and re-layouts  5.3 us

profile of v6, /device:TPU:1, one launch (start us, length us, event | category | flops | bytes accessed | tf_op | source)
XLA Modules:
  0.0 158.6 jit_solution(9555174472331190368)
XLA Ops:
  0.6 0.0 copy-start.1
  0.6 0.7 copy-done.1
  1.3 0.1 copy.11
  1.4 0.1 eq.15
  1.5 0.3 convert_reduce_fusion
  1.8 0.1 reshape.24
  1.9 0.0 copy-start.3
  1.9 0.1 copy.12
  2.0 0.6 copy-done.3
  2.6 0.6 pad.4.code_ref
  3.2 151.4 %step.1 = (bf16[512,1024]{1,0:T(8,128)(2,1)}, bf16[8,128,512]{2,1,0:T(8,128)(2,1)}, f32[8,128]{1,0:T(8,128)}) custom-call(bf16[128,512]{1,0:T(8,128)(2,1)} %x_ref.1, bf16[16,128]{1,0:T(8,128)(2,1)} %pad.4.code_ref, f32[8,1,128]{2,1,0:T(1,128)} %bitcast.8, bf16[512,1024]{1,0:T(8,128)(2,1)} %enc_ref.1, bf16[8,128,512]{2,1,0:T(8,128)(2,1)} %bitcast.6), custom_call_target="tpu_custom_call" | custom-call | tf_op jit(solution)/shard_map/step/pallas_call | solution.py:565
  154.6 0.0 copy-start
  154.6 2.4 %copy.16 = bf16[512,1024]{1,0:T(8,128)(2,1)} copy(bf16[512,1024]{1,0:T(8,128)(2,1)} %get-tuple-element.14) | data formatting | bytes 2097152
  157.0 0.0 copy-done
  157.0 0.0 copy-start.2
  157.0 1.0 copy.17
  158.0 0.0 copy-done.2
  158.0 0.6 copy.18
  (2 shorter events, 0.0 us)
Async XLA Ops:
  0.6 0.7 copy-start.1
  1.9 0.7 copy-start.3
  154.6 2.4 %copy-start = (bf16[8,128,512]{2,1,0:T(8,128)(2,1)S(1)}, bf16[8,128,512]{2,1,0:T(8,128)(2,1)}, u32[]{:S(2)}) copy-start(bf16[8,128,512]{2,1,0:T(8,128)(2,1)} %get-tuple-element.7) | copy-start | bytes 3145732
  157.0 1.0 copy-start.2
